TPU v7x, 128 devices: a whole 4x4x4 slice. The times are simulated.
128 devices in a mesh: lat: 8 (over z, x_lo), lon: 16 (over y, x_hi, core).
Axes of the slice: x: 4 (x_hi: 2, x_lo: 2; x = x_hi * 2 + x_lo), y: 4, z: 4, core: 2. Of those that a mesh axis runs over, the one named last changes fastest.
Arguments:
- features: bfloat16 [128, 512, 768], P('lat', 'lon'), may hold values from -10 to 10
- grad_output: bfloat16 [128, 512, 768], P('lat', 'lon'), may hold values from -6 to 6
- qkv_weight: bfloat16 [768, 2304], P(('lat', 'lon')), may hold values from -0.5 to 0.5
- out_weight: bfloat16 [768, 768], P(('lat', 'lon')), may hold values from -0.21875 to 0.21875
Outputs:
- grad_features: bfloat16 [128, 512, 768], P('lat', 'lon')
- grad_qkv_weight: float32 [768, 2304], P(('lat', 'lon'))
- grad_out_weight: float32 [768, 768], P(('lat', 'lon'))
All inputs are finite; a program needn't handle non-finite values.
Results may differ from a plain program's by a relative error of at most 0.018.
Values may be sent and summed in bfloat16 or wider, within the bound.
A program may use at most 128 MiB of HBM per device.

v0:
```python
import math

import jax
import jax.numpy as jnp
from jax import lax
from jax.sharding import PartitionSpec as P

HEADS = 12
RADIUS = 6
QROWS = 16
QCOLS = 16


heads_together = 2


def shifted(value, axis, steps):
    count = lax.axis_size(axis)
    pairs = [(source, (source + steps) % count) for source in range(count)]
    return lax.ppermute(value, axis, pairs)


def shifted_2(value, axis, steps):
    count = lax.axis_size(axis)
    leading, last = (max(0, -steps), min(count, count - steps))
    return lax.ppermute(value, axis, [(source, source + steps) for source in range(leading, last)])


def padded(array, sides, width, wrap):
    for axis, dim in sides:
        devices, length = (lax.axis_size(axis), array.shape[dim])
        up = [(i, (i + 1) % devices) for i in range(devices if wrap else devices - 1)]
        down = [(j, i) for i, j in up]
        last = lax.slice_in_dim(array, length - width, length, axis=dim)
        leading = lax.slice_in_dim(array, 0, width, axis=dim)
        before = lax.ppermute(last, axis, up)
        after = lax.ppermute(leading, axis, down)
        array = jnp.concatenate([before, array, after], axis=dim)
    return array


def window_mask(row_first, query_rows, query_cols, key_rows, key_cols, radius, total_rows):
    q_rows = row_first + jnp.arange(query_rows, dtype=jnp.int32)
    k_rows = row_first - radius + jnp.arange(key_rows, dtype=jnp.int32)
    row_start = jnp.clip(q_rows - radius, 0, total_rows - 2 * radius - 1)
    row_valid = (k_rows[None, :] >= row_start[:, None]) & (
        k_rows[None, :] <= row_start[:, None] + 2 * radius
    )
    q_cols = jnp.arange(query_cols, dtype=jnp.int32)
    k_cols = jnp.arange(key_cols, dtype=jnp.int32)
    col_valid = (k_cols[None, :] >= q_cols[:, None]) & (
        k_cols[None, :] <= q_cols[:, None] + 2 * radius
    )
    allowed = row_valid[:, None, :, None] & col_valid[None, :, None, :]
    return allowed.reshape(query_rows * query_cols, key_rows * key_cols)


def tile_terms(queries, keys, values, grad_heads, window, head_count, head_dim):
    q_count = queries.shape[0]
    k_count = keys.shape[0]
    softmax_scale = 1.0 / math.sqrt(head_dim)
    query_h = queries.reshape(q_count, head_count, head_dim)
    key_h = keys.reshape(k_count, head_count, head_dim)
    value_h = values.reshape(k_count, head_count, head_dim)
    grad_h = grad_heads.reshape(q_count, head_count, head_dim)
    scores = (
        jnp.einsum("qhe,khe->hqk", query_h, key_h, preferred_element_type=jnp.float32)
        * softmax_scale
    )
    scores = jnp.where(window[None], scores, -jnp.inf)
    row_max = jnp.max(scores, axis=2, keepdims=True)
    exp_terms = jnp.exp(scores - row_max)
    prob_f32 = exp_terms / jnp.sum(exp_terms, axis=2, keepdims=True)
    prob_b16 = prob_f32.astype(jnp.bfloat16)
    attended = jnp.einsum(
        "hqk,khe->qhe", prob_b16, value_h, preferred_element_type=jnp.float32
    ).astype(jnp.bfloat16)
    row_term = jnp.sum(grad_h.astype(jnp.float32) * attended.astype(jnp.float32), axis=2)
    dprob = jnp.einsum("qhe,khe->hqk", grad_h, value_h, preferred_element_type=jnp.float32)
    dscore = (prob_f32 * (dprob - row_term.T[:, :, None])).astype(jnp.bfloat16)
    grad_query = jnp.einsum("hqk,khe->qhe", dscore, key_h, preferred_element_type=jnp.float32)
    grad_key = jnp.einsum("hqk,qhe->khe", dscore, query_h, preferred_element_type=jnp.float32)
    grad_value = jnp.einsum("hqk,qhe->khe", prob_b16, grad_h, preferred_element_type=jnp.float32)
    model_part = head_count * head_dim
    return (
        attended.reshape(q_count, model_part),
        grad_query.reshape(q_count, model_part),
        grad_key.reshape(k_count, model_part),
        grad_value.reshape(k_count, model_part),
    )


def turn_lon(strip_part, offset):
    return shifted(strip_part.astype(jnp.bfloat16), "lon", offset).astype(strip_part.dtype)


def turn_lat(strip_part, offset):
    return shifted_2(strip_part.astype(jnp.bfloat16), "lat", offset).astype(strip_part.dtype)


def shards(features, grad_output, qkv_weight, out_weight):
    lat_rows, lon_cols, model_width = features.shape
    radius = RADIUS
    head_dim = model_width // HEADS
    qkv_full, out_full = (
        lax.all_gather(qkv_weight, ("lat", "lon"), axis=0, tiled=True),
        lax.all_gather(out_weight, ("lat", "lon"), axis=0, tiled=True),
    )
    x_rows = features.reshape(-1, model_width)
    grad_rows = grad_output.reshape(-1, model_width)
    projected = jnp.dot(x_rows, qkv_full, preferred_element_type=jnp.float32).astype(jnp.bfloat16)
    projected = projected.reshape(lat_rows, lon_cols, 3 * model_width)
    grad_attn = lax.dot_general(
        grad_rows, out_full, (((1,), (1,)), ((), ())), preferred_element_type=jnp.float32
    )
    grad_attn = grad_attn.astype(jnp.bfloat16).reshape(lat_rows, lon_cols, model_width)
    queries = projected[..., :model_width]
    key_value = projected[..., model_width:]
    lon_wide = padded(key_value, (("lon", 1),), radius, True)
    extended = padded(lon_wide, (("lat", 0),), radius, False)
    total_rows = lat_rows * lax.axis_size("lat")
    lat_first = lax.axis_index("lat") * lat_rows
    key_rows = QROWS + 2 * radius
    key_cols = QCOLS + 2 * radius
    wide_cols = lon_cols + 2 * radius
    grad_kv = jnp.zeros((lat_rows + 2 * radius, wide_cols, 2 * model_width), jnp.float32)
    window = window_mask(lat_first + 0, QROWS, QCOLS, key_rows, key_cols, radius, total_rows)
    out_row = []
    query_row = []
    for col_index in range(lon_cols // QCOLS):
        left_col = col_index * QCOLS
        q_tile = queries[0:QROWS, left_col : left_col + QCOLS].reshape(-1, model_width)
        g_tile = grad_attn[0:QROWS, left_col : left_col + QCOLS].reshape(-1, model_width)
        kv_tile = extended[0:key_rows, left_col : left_col + key_cols].reshape(-1, 2 * model_width)
        out_parts, query_parts, key_parts, value_parts = ([], [], [], [])
        for first_head in range(0, HEADS, heads_together):
            col_low = first_head * head_dim
            col_high = col_low + heads_together * head_dim
            attended, grad_query, grad_key, grad_value = tile_terms(
                q_tile[:, col_low:col_high],
                kv_tile[:, col_low:col_high],
                kv_tile[:, model_width + col_low : model_width + col_high],
                g_tile[:, col_low:col_high],
                window,
                heads_together,
                head_dim,
            )
            out_parts.append(attended)
            query_parts.append(grad_query)
            key_parts.append(grad_key)
            value_parts.append(grad_value)
        out_row.append(jnp.concatenate(out_parts, axis=1).reshape(QROWS, QCOLS, model_width))
        query_row.append(jnp.concatenate(query_parts, axis=1).reshape(QROWS, QCOLS, model_width))
        key_part = jnp.concatenate(key_parts + value_parts, axis=1).reshape(
            key_rows, key_cols, 2 * model_width
        )
        grad_kv = grad_kv.at[0:key_rows, left_col : left_col + key_cols].add(key_part)
    out_blocks = jnp.concatenate(out_row, axis=1)
    query_blocks = jnp.concatenate(query_row, axis=1)
    from_right = turn_lon(grad_kv[:, :radius], -1)
    from_left = turn_lon(grad_kv[:, wide_cols - radius :], 1)
    middle = grad_kv[:, radius : radius + lon_cols]
    middle = middle.at[:, :radius].add(from_left)
    middle = middle.at[:, lon_cols - radius :].add(from_right)
    from_below = turn_lat(middle[:radius], -1)
    from_above = turn_lat(middle[lat_rows + radius :], 1)
    interior = middle[radius : radius + lat_rows]
    interior = interior.at[:radius].add(from_above)
    interior = interior.at[lat_rows - radius :].add(from_below)
    softmax_scale = 1.0 / math.sqrt(head_dim)
    query_all = query_blocks.reshape(-1, model_width)
    grad_query = (query_all * softmax_scale).astype(jnp.bfloat16)
    grad_key = (
        (interior[..., :model_width] * softmax_scale).astype(jnp.bfloat16).reshape(-1, model_width)
    )
    grad_value = interior[..., model_width:].astype(jnp.bfloat16).reshape(-1, model_width)
    grad_proj = jnp.concatenate([grad_query, grad_key, grad_value], axis=1)
    attended_rows = out_blocks.reshape(-1, model_width)
    grad_features = lax.dot_general(
        grad_proj, qkv_full, (((1,), (1,)), ((), ())), preferred_element_type=jnp.float32
    )
    grad_features = grad_features.astype(jnp.bfloat16).reshape(lat_rows, lon_cols, model_width)
    first_term = lax.dot_general(
        x_rows, grad_proj, (((0,), (0,)), ((), ())), preferred_element_type=jnp.float32
    )
    second_term = lax.dot_general(
        attended_rows, grad_rows, (((0,), (0,)), ((), ())), preferred_element_type=jnp.float32
    )
    my_grads = lax.psum_scatter(
        jnp.concatenate([first_term, second_term], axis=1),
        ("lat", "lon"),
        scatter_dimension=0,
        tiled=True,
    )
    return (grad_features, my_grads[:, : 3 * model_width], my_grads[:, 3 * model_width :])


def solution(mesh):
    placed = (
        P("lat", "lon", None),
        P("lat", "lon", None),
        P(("lat", "lon"), None),
        P(("lat", "lon"), None),
    )
    return jax.shard_map(
        shards,
        mesh=mesh,
        in_specs=placed,
        out_specs=(P("lat", "lon", None), P(("lat", "lon"), None), P(("lat", "lon"), None)),
        check_vma=False,
    )
```

profile of v0, /device:TPU:1, one launch (start us, length us, event | category | flops | bytes accessed | tf_op | source)
XLA Modules:
  0.0 1026.2 jit_solution(18377570423413452368)
XLA Ops:
  9.5 3.4 and.58
  13.8 194.4 %all-gather.7.cloned.1.call-done = bf16[128,6,768]{2,1,0:T(8,128)(2,1)} async-done(((bf16[1,6,768]{2,1,0:T(8,128)(2,1)}), bf16[128,6,768]{2,1,0:T(8,128)(2,1)}) %all-gather.7.cloned.1.call-update) | async-done | bytes 1179664 | tf_op jit(solution)/shard_map/all_gather | solution.py:107
  208.2 2.3 reshape.734
  212.3 194.4 %all-gather.5.cloned.1.call-done = bf16[128,6,2304]{2,1,0:T(8,128)(2,1)} async-done(((bf16[1,6,2304]{2,1,0:T(8,128)(2,1)}), bf16[128,6,2304]{2,1,0:T(8,128)(2,1)}) %all-gather.5.cloned.1.call-update) | async-done | bytes 3538960 | tf_op jit(solution)/shard_map/all_gather | solution.py:106
  406.7 6.6 reshape.732
  413.3 4.0 convolution_convert_fusion
  417.4 2.9 collective-permute-start
  420.6 4.8 collective-permute-done
  425.4 6.1 collective-permute-done.1
  433.4 3.5 collective-permute-start.2
  475.8 3.0 pad_maximum_fusion.1
  478.8 2.2 fusion.95
  480.9 4.8 reshape.701
  485.7 3.2 fusion.97
  492.5 2.9 exponential_reduce_fusion.4
  504.6 2.9 exponential_reduce_fusion.5
  516.9 2.9 exponential_reduce_fusion.3
  529.1 2.9 exponential_reduce_fusion.2
  544.2 3.1 fusion.98
  562.8 2.4 exponential_reduce_fusion.9
  573.4 3.3 exponential_reduce_fusion.8
  584.9 3.4 exponential_reduce_fusion.7
  596.5 3.4 exponential_reduce_fusion.6
  599.9 2.0 fusion.48
  638.4 2.1 copy.241
  643.0 2.1 copy.243
  645.1 2.4 concatenate.182
  648.8 2.4 concatenate.183
  653.2 2.4 concatenate.184
  701.6 2.2 copy.239
  703.8 2.4 concatenate.177
  706.2 2.1 copy.240
  708.2 2.4 concatenate.178
  711.5 2.1 constant_dynamic-update-slice_fusion.33
  727.5 2.8 constant_dynamic-update-slice_fusion.48
  730.3 2.5 slice.521
  775.0 6.3 slice.492
  785.7 2.4 slice_add_fusion.2
  788.1 7.2 scatter-add.24
  797.0 6.4 scatter-add.25
  803.4 2.9 convert.15
  807.6 4.3 collective-permute-start.6
  819.6 13.0 %collective-permute-done.7 = bf16[6,32,1536]{2,1,0:T(8,128)(2,1)S(1)} collective-permute-done((bf16[6,32,1536]{2,1,0:T(8,128)(2,1)}, bf16[6,32,1536]{2,1,0:T(8,128)(2,1)S(1)}, u32[]{:S(2)}, u32[]{:S(2)}) %collective-permute-start.7) | collective-permute-done | bytes 589856 | tf_op jit(solution)/shard_map/ppermute | solution.py:26
  834.1 4.9 convolution_bitcast_fusion
  839.0 7.2 pad_maximum_fusion
  846.3 5.2 convolution_convert_fusion.2
  851.4 162.9 %all-reduce.4.cloned.1.call-done = f32[768,3072]{0,1:T(8,128)} async-done(((f32[768,3072]{0,1:T(8,128)}), f32[768,3072]{0,1:T(8,128)}) %all-reduce.4.cloned.1.call-update) | async-done | bytes 9437200
  1014.4 2.0 constant_dynamic-slice_fusion
  (643 shorter events, 292.8 us)
Async XLA Ops:
  7.2 406.1 %copy-start = (bf16[16,32,768]{2,1,0:T(8,128)(2,1)S(1)}, bf16[16,32,768]{2,1,0:T(8,128)(2,1)}, u32[]{:S(2)}) copy-start(bf16[16,32,768]{2,1,0:T(8,128)(2,1)} %param.16) | copy-start | bytes 2359300
  7.2 201.1 %all-gather.7.cloned.1.call-start = ((), (), s32[]{:S(2)}) async-start(), calls=%async_computation.1 | async-start | bytes 1585152 | tf_op jit(solution)/shard_map/all_gather | solution.py:107
  7.9 398.8 %all-gather.5.cloned.1.call-start = ((), (), s32[]{:S(2)}) async-start(), calls=%async_computation | async-start | bytes 4755456 | tf_op jit(solution)/shard_map/all_gather | solution.py:106
  8.7 1005.7 %all-reduce.4.cloned.1.call-start = ((), (), s32[]{:S(2)}) async-start(), calls=%async_computation.2 | async-start | bytes 18874368
  12.8 197.7 %copy-start.87 = (bf16[16,32,768]{2,1,0:T(8,128)(2,1)S(1)}, bf16[16,32,768]{2,1,0:T(8,128)(2,1)}, u32[]{:S(2)}) copy-start(bf16[16,32,768]{2,1,0:T(8,128)(2,1)} %param.17) | copy-start | bytes 2359300
  417.4 8.0 collective-permute-start
  420.3 11.2 %collective-permute-start.1 = (bf16[16,6,1536]{2,1,0:T(8,128)(2,1)S(1)}, bf16[16,6,1536]{2,1,0:T(8,128)(2,1)S(1)}, u32[]{:S(2)}, u32[]{:S(2)}) collective-permute-start(bf16[16,6,1536]{2,1,0:T(8,128)(2,1)S(1)} %get-tuple-element.119), channel_id=1, source_target_pairs={{1,0},{2,1},{3,2},{4,3},{5,4},{6,5},{7,6},{8,7},{9,8},{10,9},{11,1... | collective-permute-start | bytes 884744 | tf_op jit(solution)/shard_map/ppermute | solution.py:37
  433.4 40.9 %collective-permute-start.2 = (bf16[6,44,1536]{2,1,0:T(8,128)(2,1)}, bf16[6,44,1536]{2,1,0:T(8,128)(2,1)}, u32[]{:S(2)}, u32[]{:S(2)}) collective-permute-start(bf16[6,44,1536]{2,1,0:T(8,128)(2,1)} %get-tuple-element.116), channel_id=1, source_target_pairs={{0,16},{16,32},{32,48},{48,64},{64,80},{80,96},{96,112},{1,17},{17... | collective-permute-start | bytes 2433032 | tf_op jit(solution)/shard_map/ppermute | solution.py:36
  436.9 38.9 %collective-permute-start.3 = (bf16[6,44,1536]{2,1,0:T(8,128)(2,1)}, bf16[6,44,1536]{2,1,0:T(8,128)(2,1)}, u32[]{:S(2)}, u32[]{:S(2)}) collective-permute-start(bf16[6,44,1536]{2,1,0:T(8,128)(2,1)} %get-tuple-element.117), channel_id=1, source_target_pairs={{16,0},{32,16},{48,32},{64,48},{80,64},{96,80},{112,96},{17,1},{33... | collective-permute-start | bytes 2433032 | tf_op jit(solution)/shard_map/ppermute | solution.py:37
  568.4 4.9 copy-start.144
  580.0 4.9 copy-start.142
  635.5 20.0 %copy-start.14 = (bf16[2,256,784]{1,2,0:T(8,128)(2,1)}, bf16[2,256,784]{1,2,0:T(8,128)(2,1)S(1)}, u32[]{:S(2)}) copy-start(bf16[2,256,784]{1,2,0:T(8,128)(2,1)S(1)} %multiply_convert_fusion) | copy-start | bytes 2408452
  643.0 4.6 copy-start.39
  662.2 4.4 copy-start.37
  694.9 4.4 copy-start.42
  701.6 19.9 %slice-start = ((s8[5505024]{0:T(1024)(128)(4,1)}), s8[1310720]{0:T(1024)(128)(4,1)S(1)}, s32[]{:S(2)}) async-start(s8[5505024]{0:T(1024)(128)(4,1)} %bitcast.341), calls=%async_computation.3 | async-start | bytes 2621440
  711.5 4.7 copy-start.19
  711.5 5.6 copy-start.20
  711.5 6.4 copy-start.21
  711.5 7.3 copy-start.22
  713.6 7.9 slice-start.1
  733.8 51.9 %collective-permute-start.4 = (bf16[28,6,1536]{2,0,1:T(8,128)(2,1)}, bf16[28,6,1536]{2,0,1:T(8,128)(2,1)}, u32[]{:S(2)}, u32[]{:S(2)}) collective-permute-start(bf16[28,6,1536]{2,0,1:T(8,128)(2,1)} %copy.253), channel_id=1, source_target_pairs={{0,1},{1,2},{2,3},{3,4},{4,5},{5,6},{6,7},{7,8},{8,9},{9,10},{10,1... | collective-permute-start | bytes 1548296 | tf_op jit(solution)/shard_map/ppermute | solution.py:20
  734.9 18.0 %copy-start.124 = (bf16[256,2,64]{0,2,1:T(8,128)(2,1)S(1)}, bf16[256,2,64]{0,2,1:T(8,128)(2,1)}, u32[]{:S(2)}) copy-start(bf16[256,2,64]{0,2,1:T(8,128)(2,1)} %get-tuple-element.177) | copy-start | bytes 196612
  734.9 60.3 %collective-permute-start.5 = (bf16[28,6,1536]{2,0,1:T(8,128)(2,1)}, bf16[28,6,1536]{2,0,1:T(8,128)(2,1)S(1)}, u32[]{:S(2)}, u32[]{:S(2)}) collective-permute-start(bf16[28,6,1536]{2,0,1:T(8,128)(2,1)} %copy.255), channel_id=1, source_target_pairs={{0,15},{1,0},{2,1},{3,2},{4,3},{5,4},{6,5},{7,6},{8,7},{9,8},{10,9... | collective-permute-start | bytes 1548296 | tf_op jit(solution)/shard_map/ppermute | solution.py:20
  738.3 26.9 %copy-start.56 = (f32[16,16,768]{2,1,0:T(8,128)S(1)}, f32[16,16,768]{2,1,0:T(8,128)}, u32[]{:S(2)}) copy-start(f32[16,16,768]{2,1,0:T(8,128)} %constant_dynamic-update-slice_fusion.5) | copy-start | bytes 2359300
  738.3 26.9 %copy-start.121 = (f32[16,16,128]{2,1,0:T(8,128)S(1)}, f32[16,16,128]{2,1,0:T(8,128)}, u32[]{:S(2)}) copy-start(f32[16,16,128]{2,1,0:T(8,128)} %concatenate.153) | copy-start | bytes 393220
  755.4 16.9 %copy-start.129 = (bf16[16,16,128]{2,1,0:T(8,128)(2,1)S(1)}, bf16[16,16,128]{2,1,0:T(8,128)(2,1)}, u32[]{:S(2)}) copy-start(bf16[16,16,128]{2,1,0:T(8,128)(2,1)} %concatenate.195) | copy-start | bytes 196612
  765.2 5.7 copy-start.122
  765.2 6.3 copy-start.123
  765.2 7.0 copy-start.130
  765.3 7.1 copy-start.131
  765.3 7.1 copy-start.132
  765.3 7.1 copy-start.133
  765.3 7.1 copy-start.134
  765.3 7.8 copy-start.135
  765.3 8.4 copy-start.136
  765.3 9.1 copy-start.137
  769.2 5.8 copy-start.57
  775.0 6.4 copy-start.128
  775.0 8.8 copy-start.61
  806.3 5.5 copy-start.138
  806.4 6.1 copy-start.120
  806.4 6.4 copy-start.119
  806.4 6.8 copy-start.59
  807.6 5.6 copy-start.88
  807.6 5.7 copy-start.108
  807.6 10.9 %collective-permute-start.6 = (bf16[6,32,1536]{2,1,0:T(8,128)(2,1)}, bf16[6,32,1536]{2,1,0:T(8,128)(2,1)}, u32[]{:S(2)}, u32[]{:S(2)}) collective-permute-start(bf16[6,32,1536]{2,1,0:T(8,128)(2,1)} %get-tuple-element.89), channel_id=1, source_target_pairs={{0,16},{16,32},{32,48},{48,64},{64,80},{80,96},{96,112},{1,17},{17... | collective-permute-start | bytes 1769480 | tf_op jit(solution)/shard_map/ppermute | solution.py:26
  815.2 17.4 %collective-permute-start.7 = (bf16[6,32,1536]{2,1,0:T(8,128)(2,1)}, bf16[6,32,1536]{2,1,0:T(8,128)(2,1)S(1)}, u32[]{:S(2)}, u32[]{:S(2)}) collective-permute-start(bf16[6,32,1536]{2,1,0:T(8,128)(2,1)} %get-tuple-element.88), channel_id=1, source_target_pairs={{16,0},{32,16},{48,32},{64,48},{80,64},{96,80},{112,96},{17,1},{33... | collective-permute-start | bytes 1769480 | tf_op jit(solution)/shard_map/ppermute | solution.py:26
  (130 other events, 306.0 us)
Sparse Core Ops, SparseCore 0:
  9.7 198.4 all-gather.6
  210.0 196.7 all-gather.4
  846.4 167.9 all-reduce.3
where the time goes:
time: 1040 us; the launch traced here: 1030 us
  waiting for transfers between devices  580 us (56%)
  local copies, waits for them, and re-layouts  268 us (26%)
  matrix products  103 us (10%)
  other arithmetic  44.1 us (4%)
  between operations  15.9 us (2%)
  starting transfers between devices  14.7 us (1%)
    all_gather x1, waiting for transfers between devices, shards(): lax.all_gather(qkv_weight, ('lat', 'lon'), axis=0, tiled=True)  194 us
    all_gather x1, waiting for transfers between devices, shards(): lax.all_gather(out_weight, ('lat', 'lon'), axis=0, tiled=True)  194 us
    unnamed x4, waiting for transfers between devices  164 us
    unnamed x428, local copies, waits for them, and re-layouts  101 us
    concatenate x26, local copies, waits for them, and re-layouts, shards(): jnp.concatenate(key_parts + value_parts, axis=1)  36.7 us
    sub x12, matrix products, tile_terms(): exp_terms = jnp.exp(scores - row_max)  29.7 us
  transfers between devices with their start and end apart: 11, of which 8 were waited for; matrix products, arithmetic and copies ran while one was open for 11% of the time, Pallas kernels for 0%

commit v1 on v0

--- a/solution.py
+++ b/solution.py
@@ -1,9 +1,331 @@
+import functools
 import math
 
 import jax
 import jax.numpy as jnp
 from jax import lax
+from jax.experimental import pallas as pl
+from jax.experimental.pallas import tpu as pltpu
 from jax.sharding import PartitionSpec as P
+
+MESH = pl.DeviceIdType.MESH
+BF = jnp.bfloat16
+F32 = jnp.float32
+
+
+def place():
+    lat = lax.axis_index("lat")
+    lon = lax.axis_index("lon")
+    z, x_lo = lat // 2, lat % 2
+    y, x_hi, core = lon // 4, (lon // 2) % 2, lon % 2
+    return {"z": z, "y": y, "x": x_hi * 2 + x_lo}, core
+
+
+def device(at, core):
+    return (at["z"] * 2 + at["x"] % 2, at["y"] * 4 + (at["x"] // 2) * 2 + core)
+
+
+def moved(at, axis, steps):
+    out = dict(at)
+    out[axis] = (at[axis] + steps + 4) % 4
+    return out
+
+
+def meet(peers):
+    barrier = pltpu.get_barrier_semaphore()
+    for peer in peers:
+        pl.semaphore_signal(barrier, inc=1, device_id=peer, device_id_type=MESH)
+    pl.semaphore_wait(barrier, len(peers))
+
+
+def torus_peers(at, core):
+    peers = [device(at, 1 - core)]
+    for axis in ("z", "y", "x"):
+        for steps in (1, -1):
+            peers.append(device(moved(at, axis, steps), core))
+    return peers
+
+
+ORDERS = (("x", "y", "z"), ("y", "z", "x"), ("z", "x", "y"))
+
+
+def region(at, full, axis=None, coord=None):
+    index = []
+    for name in ("z", "y", "x"):
+        if name == axis:
+            index.append(coord)
+        elif name in full:
+            index.append(slice(None))
+        else:
+            index.append(at[name])
+    return tuple(index)
+
+
+def send(src, dst, ssem, rsem, peer):
+    copy = pltpu.make_async_remote_copy(
+        src_ref=src, dst_ref=dst, send_sem=ssem, recv_sem=rsem, device_id=peer, device_id_type=MESH
+    )
+    copy.start()
+    return copy
+
+
+def unpack(blocks, write):
+    def body(step, carry):
+        z, rest = step // 4, step % 4
+        x_lo, y_pair = rest // 2, rest % 2
+        for part in range(3):
+            for parity in range(2):
+                pieces = []
+                for y in range(2):
+                    for x_hi in range(2):
+                        for core in range(2):
+                            piece = blocks[part, parity, z, 2 * y_pair + y, 2 * x_hi + x_lo, core]
+                            pieces.append(piece.astype(F32).reshape(24, 128))
+                for chunk in range(4):
+                    rows = jnp.concatenate([p[6 * chunk : 6 * chunk + 6] for p in pieces], axis=0)
+                    write(step, 8 * part + 4 * parity + chunk, rows.astype(BF))
+        return carry
+
+    lax.fori_loop(0, 16, body, 0)
+
+
+def gather(own):
+    def kernel(own_ref, qkv_ref, out_ref, blocks, ssem, rsem, psem, local_sem):
+        at, core = place()
+        meet(torus_peers(at, core))
+        partner = device(at, 1 - core)
+        z, y, x = at["z"], at["y"], at["x"]
+        local = pltpu.make_async_copy(own_ref.at[:, core], blocks.at[:, core, z, y, x, core], local_sem)
+        local.start()
+        pair = send(
+            own_ref.at[:, 1 - core], blocks.at[:, 1 - core, z, y, x, core], psem.at[0, 0], psem.at[1, 0], partner
+        )
+        local.wait()
+        pair.wait_recv()
+        sent = [pair]
+        lasts = []
+        for stage in range(3):
+            whole, rounds = {}, {}
+            for part in range(3):
+                axis, full = ORDERS[part][stage], ORDERS[part][:stage]
+                for k, steps in ((0, 1), (1, -1)):
+                    where = (part, core) + region(at, full, axis, at[axis])
+                    whole[part, k] = send(
+                        blocks.at[where], blocks.at[where], ssem.at[part, stage, k], rsem.at[part, stage, k],
+                        device(moved(at, axis, steps), core),
+                    )
+            for part in range(3):
+                axis, full = ORDERS[part][stage], ORDERS[part][:stage]
+                for k, steps in ((0, 1), (1, -1)):
+                    whole[part, k].wait_recv()
+                    back = (at[axis] - steps + 4) % 4
+                    where = (part, core) + region(at, full, axis, back) + (k,)
+                    rounds[part, k] = send(
+                        blocks.at[where], blocks.at[where], ssem.at[part, stage, 2 + k],
+                        rsem.at[part, stage, 2 + k], device(moved(at, axis, steps), core),
+                    )
+            for part in range(3):
+                for k in range(2):
+                    rounds[part, k].wait_recv()
+                    sent += [whole[part, k], rounds[part, k]]
+                if stage == 2:
+                    lasts.append(
+                        send(
+                            blocks.at[part, core], blocks.at[part, core], psem.at[0, 1 + part],
+                            psem.at[1, 1 + part], partner,
+                        )
+                    )
+        for copy in lasts:
+            copy.wait_recv()
+        for copy in sent + lasts:
+            copy.wait_send()
+
+        def write(step, chunk, rows):
+            first = pl.multiple_of(step * 48, 16)
+            if chunk < 18:
+                qkv_ref[pl.ds(first, 48), 128 * chunk : 128 * chunk + 128] = rows
+            else:
+                chunk -= 18
+                out_ref[pl.ds(first, 48), 128 * chunk : 128 * chunk + 128] = rows
+
+        unpack(blocks, write)
+
+    vmem = pl.BlockSpec(memory_space=pltpu.VMEM)
+    return pl.pallas_call(
+        kernel,
+        out_shape=(jax.ShapeDtypeStruct((768, 2304), BF), jax.ShapeDtypeStruct((768, 768), BF)),
+        in_specs=[vmem],
+        out_specs=(vmem, vmem),
+        scratch_shapes=[
+            pltpu.VMEM((3, 2, 4, 4, 4, 2, 3, 8, 128), BF),
+            pltpu.SemaphoreType.DMA((3, 3, 4)),
+            pltpu.SemaphoreType.DMA((3, 3, 4)),
+            pltpu.SemaphoreType.DMA((2, 4)),
+            pltpu.SemaphoreType.DMA,
+        ],
+        compiler_params=pltpu.CompilerParams(collective_id=0, has_side_effects=True),
+        name="gather_weights",
+    )(own)
+
+
+def to_blocks(qkv, out):
+    rows = jnp.concatenate([qkv, out], axis=1)
+    rows = rows.reshape(6, 6, 4, 128).transpose(1, 2, 0, 3)
+    return rows.reshape(3, 2, 3, 8, 128)
+
+
+def from_blocks(blocks):
+    rows = blocks.reshape(6, 4, 6, 128).transpose(2, 0, 1, 3)
+    return rows.reshape(6, 3072)
+
+
+def scatter(first, second):
+    def kernel(
+        qkv_ref, out_ref, own_ref, blocks, pair_in, half0, whole0, half1, whole1, half2, whole2, last_out, last_in,
+        ssem, rsem, psem,
+    ):
+        at, core = place()
+        meet(torus_peers(at, core))
+        partner = device(at, 1 - core)
+        halves, wholes = (half0, half1, half2), (whole0, whole1, whole2)
+        sent = []
+
+        def pack(part):
+            def body(step, carry):
+                z, rest = step // 4, step % 4
+                x_lo, y_pair = rest // 2, rest % 2
+                first_row = pl.multiple_of(step * 48, 16)
+                for parity in range(2):
+                    chunks = []
+                    for q in range(4):
+                        c = 8 * part + 4 * parity + q
+                        ref, c = (qkv_ref, c) if c < 18 else (out_ref, c - 18)
+                        chunks.append(ref[pl.ds(first_row, 48), 128 * c : 128 * c + 128].astype(F32))
+                    for e in range(8):
+                        y, x_hi, to = e // 4, (e // 2) % 2, e % 2
+                        rows = jnp.concatenate([c[6 * e : 6 * e + 6] for c in chunks], axis=0)
+                        blocks[part, parity, z, 2 * y_pair + y, 2 * x_hi + x_lo, to] = rows.reshape(3, 8, 128).astype(BF)
+                return carry
+
+            lax.fori_loop(0, 16, body, 0)
+
+        pairs = []
+        for part in range(3):
+            pack(part)
+            pairs.append(
+                send(blocks.at[part, 1 - core], pair_in.at[part], psem.at[0, part], psem.at[1, part], partner)
+            )
+        sent += pairs
+        for part in range(3):
+            pairs[part].wait_recv()
+
+            def add(step, carry, part=part):
+                z, rest = step // 16, step % 16
+                y, x = rest // 4, rest % 4
+                total = blocks[part, core, z, y, x].astype(F32) + pair_in[part, z, y, x].astype(F32)
+                blocks[part, core, z, y, x] = total.astype(BF)
+                return carry
+
+            lax.fori_loop(0, 64, add, 0)
+
+        def each(full, body):
+            count = len(full)
+            if count == 0:
+                body(())
+            elif count == 1:
+                lax.fori_loop(0, 4, lambda i, c: (body((i,)), c)[1], 0)
+            else:
+                lax.fori_loop(0, 16, lambda i, c: (body((i // 4, i % 4)), c)[1], 0)
+
+        def spot(part, where, inner):
+            inner = list(inner)
+            return (part, core) + tuple(inner.pop(0) if isinstance(w, slice) else w for w in where)
+
+        for stage in range(3):
+            early, late = {}, {}
+            plan = {}
+            for part in range(3):
+                order = ORDERS[part][::-1]
+                axis, full = order[stage], order[stage + 1 :]
+                plan[part] = (axis, full)
+                far = region(at, full, axis, (at[axis] + 2) % 4)
+                for k, steps in ((0, 1), (1, -1)):
+                    early[part, k] = send(
+                        blocks.at[(part, core) + far + (k,)], halves[stage].at[part, k],
+                        ssem.at[part, stage, k], rsem.at[part, stage, k], device(moved(at, axis, steps), core),
+                    )
+            for part in range(3):
+                axis, full = plan[part]
+                for k, steps in ((0, 1), (1, -1)):
+                    early[part, k].wait_recv()
+                    near = region(at, full, axis, (at[axis] + steps + 4) % 4)
+
+                    def add(inner, part=part, k=k, near=near):
+                        here = spot(part, near, inner) + (k,)
+                        total = blocks[here].astype(F32) + halves[stage][(part, k) + inner].astype(F32)
+                        blocks[here] = total.astype(BF)
+
+                    each(full, add)
+                    late[part, k] = send(
+                        blocks.at[(part, core) + near], wholes[stage].at[part, k],
+                        ssem.at[part, stage, 2 + k], rsem.at[part, stage, 2 + k], device(moved(at, axis, steps), core),
+                    )
+            for part in range(3):
+                axis, full = plan[part]
+                late[part, 0].wait_recv()
+                late[part, 1].wait_recv()
+                mine = region(at, full, axis, at[axis])
+
+                def add(inner, part=part, mine=mine):
+                    here = spot(part, mine, inner)
+                    total = blocks[here].astype(F32) + wholes[stage][(part, 0) + inner].astype(F32)
+                    total = total + wholes[stage][(part, 1) + inner].astype(F32)
+                    if stage < 2:
+                        blocks[here] = total.astype(BF)
+                    else:
+                        last_out[part] = total
+
+                each(full, add)
+                sent += [early[part, 0], early[part, 1], late[part, 0], late[part, 1]]
+        ends = []
+        for part in range(3):
+            ends.append(
+                send(last_out.at[part, 1 - core], last_in.at[part], psem.at[0, 3 + part], psem.at[1, 3 + part], partner)
+            )
+        for part in range(3):
+            own_ref[part, core] = last_out[part, core]
+        for part in range(3):
+            ends[part].wait_recv()
+            own_ref[part, 1 - core] = last_in[part]
+        for copy in sent + ends:
+            copy.wait_send()
+
+    vmem = pl.BlockSpec(memory_space=pltpu.VMEM)
+    tail = (3, 8, 128)
+    own = pl.pallas_call(
+        kernel,
+        out_shape=jax.ShapeDtypeStruct((3, 2) + tail, F32),
+        in_specs=[vmem, vmem],
+        out_specs=vmem,
+        scratch_shapes=[
+            pltpu.VMEM((3, 2, 4, 4, 4, 2) + tail, BF),
+            pltpu.VMEM((3, 4, 4, 4, 2) + tail, BF),
+            pltpu.VMEM((3, 2, 4, 4) + tail, BF),
+            pltpu.VMEM((3, 2, 4, 4, 2) + tail, BF),
+            pltpu.VMEM((3, 2, 4) + tail, BF),
+            pltpu.VMEM((3, 2, 4, 2) + tail, BF),
+            pltpu.VMEM((3, 2) + tail, BF),
+            pltpu.VMEM((3, 2, 2) + tail, BF),
+            pltpu.VMEM((3, 2) + tail, F32),
+            pltpu.VMEM((3,) + tail, F32),
+            pltpu.SemaphoreType.DMA((3, 3, 4)),
+            pltpu.SemaphoreType.DMA((3, 3, 4)),
+            pltpu.SemaphoreType.DMA((2, 6)),
+        ],
+        compiler_params=pltpu.CompilerParams(collective_id=1, has_side_effects=True, vmem_limit_bytes=60 << 20),
+        name="scatter_grads",
+    )(first, second)
+    return from_blocks(own)
 
 HEADS = 12
 RADIUS = 6
@@ -102,10 +424,7 @@
     lat_rows, lon_cols, model_width = features.shape
     radius = RADIUS
     head_dim = model_width // HEADS
-    qkv_full, out_full = (
-        lax.all_gather(qkv_weight, ("lat", "lon"), axis=0, tiled=True),
-        lax.all_gather(out_weight, ("lat", "lon"), axis=0, tiled=True),
-    )
+    qkv_full, out_full = gather(to_blocks(qkv_weight, out_weight))
     x_rows = features.reshape(-1, model_width)
     grad_rows = grad_output.reshape(-1, model_width)
     projected = jnp.dot(x_rows, qkv_full, preferred_element_type=jnp.float32).astype(jnp.bfloat16)
@@ -186,12 +505,7 @@
     second_term = lax.dot_general(
         attended_rows, grad_rows, (((0,), (0,)), ((), ())), preferred_element_type=jnp.float32
     )
-    my_grads = lax.psum_scatter(
-        jnp.concatenate([first_term, second_term], axis=1),
-        ("lat", "lon"),
-        scatter_dimension=0,
-        tiled=True,
-    )
+    my_grads = scatter(first_term, second_term)
     return (grad_features, my_grads[:, : 3 * model_width], my_grads[:, 3 * model_width :])
 
 

time: 1040 us -> 495 us (0.48)
  waiting for transfers between devices: 580 us -> 28.8 us
  Pallas kernels: 0 us -> 90.8 us
  local copies, waits for them, and re-layouts: 268 us -> 218 us
  other arithmetic: 44.1 us -> 28.5 us
  between operations: 15.9 us -> 2.94 us
    all_gather x2 -> x0, waiting for transfers between devices: 389 us -> none  [the longest x1 194 us: shards(): lax.all_gather(qkv_weight, ('lat', 'lon'), axis=0, tiled=True)]
    unnamed x4 -> x0, waiting for transfers between devices: 164 us -> none
    pallas_call x0 -> x2, Pallas kernels: none -> 90.8 us  [the longest x1 49.7 us: scatter(): pl.pallas_call(kernel, out_shape=jax.ShapeDtypeStruct((3, 2) + tail, F32)...]
    unnamed x428 -> x348, local copies, waits for them, and re-layouts: 101 us -> 77 us
  transfers between devices with their start and end apart: 11 -> 8, of which waited for: 8 -> 5; matrix products, arithmetic and copies ran while one was open for 11% -> 13% of each run, Pallas kernels for 0% -> 0%
where the time goes in v1:
time: 495 us; the launch traced here: 490 us
  local copies, waits for them, and re-layouts  218 us (44%)
  matrix products  110 us (22%)
  Pallas kernels  90.8 us (18%)
  waiting for transfers between devices  28.8 us (6%)
  other arithmetic  28.5 us (6%)
  starting transfers between devices  10.7 us (2%)
    unnamed x348, local copies, waits for them, and re-layouts  77 us
    pallas_call x1, Pallas kernels, scatter(): pl.pallas_call(kernel, out_shape=jax.ShapeDtypeStruct((3, 2) + tail, F32)...  49.7 us
    pallas_call x1, Pallas kernels, gather(): pl.pallas_call(kernel, out_shape=(jax.ShapeDtypeStruct((768, 2304), BF),...  41 us
    sub x12, matrix products, tile_terms(): exp_terms = jnp.exp(scores - row_max)  37.9 us
    concatenate x26, local copies, waits for them, and re-layouts, shards(): jnp.concatenate(key_parts + value_parts, axis=1)  27.2 us
    transpose x12, local copies, waits for them, and re-layouts, tile_terms(): jnp.einsum('hqk,qhe->khe', dscore, query_h, preferred_element_type=jnp.fl...  20 us
    transpose x12, local copies, waits for them, and re-layouts, tile_terms(): jnp.einsum('hqk,qhe->khe', prob_b16, grad_h, preferred_element_type=jnp.f...  19.7 us
    ppermute x2, waiting for transfers between devices, shifted_2(): lax.ppermute(value, axis, [(source, source + steps) for source in range(l...  15.9 us
  transfers between devices with their start and end apart: 8, of which 5 were waited for; matrix products, arithmetic and copies ran while one was open for 13% of the time, Pallas kernels for 0%

profile of v1, /device:TPU:1, one launch (start us, length us, event | category | flops | bytes accessed | tf_op | source)
XLA Modules:
  0.0 489.5 jit_solution(15934816481779137375)
XLA Ops:
  2.2 41.0 %gather_weights.1 = (bf16[768,2304]{1,0:T(8,128)(2,1)}, bf16[768,768]{1,0:T(8,128)(2,1)}) custom-call(bf16[3,2,3,8,128]{4,3,2,1,0:T(8,128)(2,1)} %reshape.683.own_ref), custom_call_target="tpu_custom_call" | custom-call | tf_op jit(solution)/shard_map/gather_weights/pallas_call | solution.py:154
  43.2 4.1 convolution_convert_fusion
  56.0 6.0 %collective-permute-done.1 = bf16[16,6,1536]{2,1,0:T(8,128)(2,1)} collective-permute-done((bf16[16,6,1536]{2,1,0:T(8,128)(2,1)}, bf16[16,6,1536]{2,1,0:T(8,128)(2,1)}, u32[]{:S(2)}, u32[]{:S(2)}) %collective-permute-start.1) | collective-permute-done | bytes 294944 | tf_op jit(solution)/shard_map/ppermute | solution.py:359
  62.0 3.0 pad_maximum_fusion.6
  65.0 3.5 collective-permute-start.2
  70.6 4.0 and.58
  74.6 1.9 copy.170
  103.0 5.2 %collective-permute-done.3 = bf16[6,44,1536]{2,1,0:T(8,128)(2,1)} collective-permute-done((bf16[6,44,1536]{2,1,0:T(8,128)(2,1)}, bf16[6,44,1536]{2,1,0:T(8,128)(2,1)}, u32[]{:S(2)}, u32[]{:S(2)}) %collective-permute-start.3) | collective-permute-done | bytes 811040 | tf_op jit(solution)/shard_map/ppermute | solution.py:359
  108.2 2.7 pad_maximum_fusion
  110.9 2.2 fusion.95
  113.1 5.1 %reshape.715 = bf16[784,1536]{1,0:T(8,128)(2,1)} reshape(bf16[28,28,1536]{2,1,0:T(8,128)(2,1)} %get-tuple-element.81) | data formatting | bytes 4816896 | tf_op jit(solution)/shard_map/reshape | solution.py:453
  118.2 3.2 fusion.97
  124.9 2.9 exponential_reduce_fusion.5
  138.2 2.9 exponential_reduce_fusion.4
  151.5 2.9 exponential_reduce_fusion.3
  164.8 2.9 exponential_reduce_fusion.2
  178.1 2.9 exponential_reduce_fusion.1
  191.4 13.1 %exponential_reduce_fusion = (f32[2,256]{1,0:T(2,128)S(1)}, f32[2,256,784]{1,2,0:T(8,128)}) fusion(bf16[256,2,64]{0,2,1:T(8,128)(2,1)} %bitcast.451, bf16[784,2,64]{0,2,1:T(8,128)(2,1)} %bitcast.360, pred[256,784]{0,1:T(8,128)(4,1)} %copy.170), kind=kOutput, calls=%fused_computation.61 | convolution fusion | flops 52986640 | bytes 2074624 | tf_op jit(solution)/shard_map/sub | solution.py:394
  213.0 3.0 fusion.98
  253.9 1.9 exponential_reduce_fusion.6
  280.8 1.8 copy.245
  283.9 1.8 copy.251
  289.6 1.8 copy.246
  292.7 1.8 copy.252
  298.5 1.8 copy.247
  301.6 2.2 copy.253
  307.8 1.8 copy.230
  310.9 1.8 copy.236
  318.3 1.8 copy.231
  325.4 1.8 copy.232
  328.5 1.8 copy.238
  332.4 1.8 copy.233
  335.5 1.8 copy.239
  339.4 1.8 copy.234
  346.4 1.8 copy.235
  349.5 2.0 copy.241
  373.0 3.3 slice.492
  383.3 2.4 slice_add_fusion.2
  385.6 7.2 %scatter-add.24 = f32[28,32,1536]{2,1,0:T(8,128)} dynamic-update-slice(f32[28,32,1536]{2,1,0:T(8,128)} %slice.492, f32[28,6,1536]{2,1,0:T(8,128)S(1)} %slice_add_fusion.2, s32[]{:T(128)} %constant.176.clone.1, s32[]{:T(128)} %constant.176.clone.1, s32[]{:T(128)} %constant.176.clone.1) | dynamic-update-slice | bytes 2064388 | tf_op jit(solution)/shard_map/scatter-add | solution.py:482
  394.6 6.4 %scatter-add.25 = f32[28,32,1536]{2,1,0:T(8,128)} dynamic-update-slice(f32[28,32,1536]{2,1,0:T(8,128)} %scatter-add.24, f32[28,6,1536]{2,1,0:T(8,128)S(1)} %slice_add_fusion.1, s32[]{:T(128)} %constant.176.clone.1, s32[]{:T(128)} %constant.182.clone.1, s32[]{:T(128)} %constant.176.clone.1) | dynamic-update-slice | bytes 2064388 | tf_op jit(solution)/shard_map/scatter-add | solution.py:483
  401.0 2.9 convert.15
  404.1 1.8 collective-permute-start.6
  405.9 3.4 convolution_bitcast_fusion.1.out_ref
  411.3 1.9 collective-permute-done.6
  413.4 13.9 %collective-permute-done.7 = bf16[6,32,1536]{2,1,0:T(8,128)(2,1)S(1)} collective-permute-done((bf16[6,32,1536]{2,1,0:T(8,128)(2,1)S(1)}, bf16[6,32,1536]{2,1,0:T(8,128)(2,1)S(1)}, u32[]{:S(2)}, u32[]{:S(2)}) %collective-permute-start.7) | collective-permute-done | bytes 589856 | tf_op jit(solution)/shard_map/ppermute | solution.py:348
  429.6 2.9 convolution_convert_fusion.2
  432.5 4.9 %convolution_bitcast_fusion.qkv_ref = f32[768,2304]{1,0:T(8,128)} fusion(bf16[512,768]{1,0:T(8,128)(2,1)S(1)} %bitcast.348, bf16[512,768]{1,0:T(8,128)(2,1)S(1)} %bitcast.407, bf16[512,768]{1,0:T(8,128)(2,1)S(1)} %bitcast.412, bf16[512,768]{1,0:T(8,128)(2,1)S(1)} %bitcast.410), kind=kOutput, calls=%fused_computation.12 | convolution fusion | flops 1819017216 | bytes 10223616 | tf_op jit(solution)/shard_map/dot_general | solution.py:502
  437.4 49.7 %scatter_grads.1 = f32[3,2,3,8,128]{4,3,2,1,0:T(8,128)} custom-call(f32[768,2304]{1,0:T(8,128)} %convolution_bitcast_fusion.qkv_ref, f32[768,768]{1,0:T(8,128)} %convolution_bitcast_fusion.1.out_ref), custom_call_target="tpu_custom_call" | custom-call | tf_op jit(solution)/shard_map/scatter_grads/pallas_call | solution.py:305
  (557 shorter events, 241.6 us)
Async XLA Ops:
  0.6 42.6 %copy-start = (bf16[16,32,768]{2,1,0:T(8,128)(2,1)S(1)}, bf16[16,32,768]{2,1,0:T(8,128)(2,1)}, u32[]{:S(2)}) copy-start(bf16[16,32,768]{2,1,0:T(8,128)(2,1)} %param.16) | copy-start | bytes 2359300
  43.2 7.8 %copy-start.124 = (bf16[768,768]{1,0:T(8,128)(2,1)S(1)}, bf16[768,768]{1,0:T(8,128)(2,1)}, u32[]{:S(2)}) copy-start(bf16[768,768]{1,0:T(8,128)(2,1)} %get-tuple-element.78) | copy-start | bytes 3538948
  43.2 7.8 %copy-start.125 = (bf16[16,32,768]{2,1,0:T(8,128)(2,1)S(1)}, bf16[16,32,768]{2,1,0:T(8,128)(2,1)}, u32[]{:S(2)}) copy-start(bf16[16,32,768]{2,1,0:T(8,128)(2,1)} %param.17) | copy-start | bytes 2359300
  49.8 6.3 %collective-permute-start = (bf16[16,6,1536]{2,1,0:T(8,128)(2,1)}, bf16[16,6,1536]{2,1,0:T(8,128)(2,1)}, u32[]{:S(2)}, u32[]{:S(2)}) collective-permute-start(bf16[16,6,1536]{2,1,0:T(8,128)(2,1)} %get-tuple-element.113), channel_id=1, source_target_pairs={{0,1},{1,2},{2,3},{3,4},{4,5},{5,6},{6,7},{7,8},{8,9},{9,10},{10,1... | collective-permute-start | bytes 884744 | tf_op jit(solution)/shard_map/ppermute | solution.py:358
  51.0 11.1 %collective-permute-start.1 = (bf16[16,6,1536]{2,1,0:T(8,128)(2,1)}, bf16[16,6,1536]{2,1,0:T(8,128)(2,1)}, u32[]{:S(2)}, u32[]{:S(2)}) collective-permute-start(bf16[16,6,1536]{2,1,0:T(8,128)(2,1)} %get-tuple-element.114), channel_id=1, source_target_pairs={{1,0},{2,1},{3,2},{4,3},{5,4},{6,5},{7,6},{8,7},{9,8},{10,9},{11,1... | collective-permute-start | bytes 884744 | tf_op jit(solution)/shard_map/ppermute | solution.py:359
  65.0 38.0 %collective-permute-start.2 = (bf16[6,44,1536]{2,1,0:T(8,128)(2,1)}, bf16[6,44,1536]{2,1,0:T(8,128)(2,1)}, u32[]{:S(2)}, u32[]{:S(2)}) collective-permute-start(bf16[6,44,1536]{2,1,0:T(8,128)(2,1)} %get-tuple-element.111), channel_id=1, source_target_pairs={{0,16},{16,32},{32,48},{48,64},{64,80},{80,96},{96,112},{1,17},{17... | collective-permute-start | bytes 2433032 | tf_op jit(solution)/shard_map/ppermute | solution.py:358
  68.5 39.7 %collective-permute-start.3 = (bf16[6,44,1536]{2,1,0:T(8,128)(2,1)}, bf16[6,44,1536]{2,1,0:T(8,128)(2,1)}, u32[]{:S(2)}, u32[]{:S(2)}) collective-permute-start(bf16[6,44,1536]{2,1,0:T(8,128)(2,1)} %get-tuple-element.112), channel_id=1, source_target_pairs={{16,0},{32,16},{48,32},{64,48},{80,64},{96,80},{112,96},{17,1},{33... | collective-permute-start | bytes 2433032 | tf_op jit(solution)/shard_map/ppermute | solution.py:359
  74.6 16.0 %copy-start.103 = (bf16[256,128]{1,0:T(8,128)(2,1)S(1)}, bf16[256,128]{1,0:T(8,128)(2,1)}, u32[]{:S(2)}) copy-start(bf16[256,128]{1,0:T(8,128)(2,1)} %get-tuple-element.132) | copy-start | bytes 196612
  213.0 3.3 copy-start.112
  261.6 3.1 copy-start.22
  264.8 3.1 copy-start.87
  265.7 3.0 copy-start.26
  267.0 3.2 copy-start.23
  271.8 4.8 copy-start.25
  275.3 2.7 copy-start.74
  282.6 4.3 copy-start.75
  291.5 4.3 copy-start.76
  300.3 4.8 copy-start.77
  310.9 4.7 copy-start.78
  320.1 4.4 copy-start.89
  327.2 4.4 copy-start.90
  334.3 4.3 copy-start.91
  341.3 4.3 copy-start.92
  364.5 8.4 %copy-start.1 = (f32[28,44,1536]{2,1,0:T(8,128)}, f32[28,44,1536]{2,1,0:T(8,128)S(1)}, u32[]{:S(2)}) copy-start(f32[28,44,1536]{2,1,0:T(8,128)S(1)} %get-tuple-element.79) | copy-start | bytes 22708228
  366.1 2.5 copy-start.33
  366.1 2.5 copy-start.79
  366.1 2.6 copy-start.93
  366.1 2.6 copy-start.120
  366.1 2.6 copy-start.80
  366.1 17.2 %collective-permute-start.4 = (bf16[28,6,1536]{2,0,1:T(8,128)(2,1)}, bf16[28,6,1536]{2,0,1:T(8,128)(2,1)}, u32[]{:S(2)}, u32[]{:S(2)}) collective-permute-start(bf16[28,6,1536]{2,0,1:T(8,128)(2,1)} %copy.254), channel_id=1, source_target_pairs={{0,1},{1,2},{2,3},{3,4},{4,5},{5,6},{6,7},{7,8},{8,9},{9,10},{10,1... | collective-permute-start | bytes 1548296 | tf_op jit(solution)/shard_map/ppermute | solution.py:342
  366.8 2.8 copy-start.34
  366.8 2.8 copy-start.84
  366.8 2.8 copy-start.98
  366.8 3.5 copy-start.99
  366.8 4.1 copy-start.100
  367.8 3.8 copy-start.101
  367.8 4.5 copy-start.102
  367.8 25.0 %collective-permute-start.5 = (bf16[28,6,1536]{2,0,1:T(8,128)(2,1)}, bf16[28,6,1536]{2,0,1:T(8,128)(2,1)S(1)}, u32[]{:S(2)}, u32[]{:S(2)}) collective-permute-start(bf16[28,6,1536]{2,0,1:T(8,128)(2,1)} %copy.256), channel_id=1, source_target_pairs={{0,15},{1,0},{2,1},{3,2},{4,3},{5,4},{6,5},{7,6},{8,7},{9,8},{10,9... | collective-permute-start | bytes 1548296 | tf_op jit(solution)/shard_map/ppermute | solution.py:342
  369.6 3.4 copy-start.121
  373.0 3.3 copy-start.68
  373.0 4.3 copy-start.69
  376.4 3.8 copy-start.70
  377.4 3.1 copy-start.85
  404.0 6.9 %slice-start = ((s8[5505024]{0:T(1024)(128)(4,1)}), s8[4194304]{0:T(1024)(128)(4,1)S(1)}, s32[]{:S(2)}) async-start(s8[5505024]{0:T(1024)(128)(4,1)} %bitcast.349), calls=%async_computation | async-start | bytes 8388608
  404.0 6.8 %copy-start.36 = (f32[16,16,768]{2,1,0:T(8,128)S(1)}, f32[16,16,768]{2,1,0:T(8,128)}, u32[]{:S(2)}) copy-start(f32[16,16,768]{2,1,0:T(8,128)} %copy-done.35) | copy-start | bytes 2359300
  404.1 6.9 %slice-start.1 = ((s8[5505024]{0:T(1024)(128)(4,1)}), s8[1310720]{0:T(1024)(128)(4,1)S(1)}, s32[]{:S(2)}) async-start(s8[5505024]{0:T(1024)(128)(4,1)} %bitcast.349), calls=%async_computation.1 | async-start | bytes 2621440
  404.1 9.2 %collective-permute-start.6 = (bf16[6,32,1536]{2,1,0:T(8,128)(2,1)S(1)}, bf16[6,32,1536]{2,1,0:T(8,128)(2,1)S(1)}, u32[]{:S(2)}, u32[]{:S(2)}) collective-permute-start(bf16[6,32,1536]{2,1,0:T(8,128)(2,1)S(1)} %get-tuple-element.84), channel_id=1, source_target_pairs={{0,16},{16,32},{32,48},{48,64},{64,80},{80,96},{96,112},{1,17},{17... | collective-permute-start | bytes 1769480 | tf_op jit(solution)/shard_map/ppermute | solution.py:348
  409.3 18.0 %collective-permute-start.7 = (bf16[6,32,1536]{2,1,0:T(8,128)(2,1)S(1)}, bf16[6,32,1536]{2,1,0:T(8,128)(2,1)S(1)}, u32[]{:S(2)}, u32[]{:S(2)}) collective-permute-start(bf16[6,32,1536]{2,1,0:T(8,128)(2,1)S(1)} %get-tuple-element.83), channel_id=1, source_target_pairs={{16,0},{32,16},{48,32},{64,48},{80,64},{96,80},{112,96},{17,1},{33... | collective-permute-start | bytes 1769480 | tf_op jit(solution)/shard_map/ppermute | solution.py:348
  (89 other events, 150.0 us)

commit v2 on v1

--- a/solution.py
+++ b/solution.py
@@ -89,14 +89,16 @@
     lax.fori_loop(0, 16, body, 0)
 
 
-def gather(own):
-    def kernel(own_ref, qkv_ref, out_ref, blocks, ssem, rsem, psem, local_sem):
+def gather(own, features):
+    def kernel(own_ref, x_ref, qkv_ref, out_ref, ext_ref, blocks, ssem, rsem, psem, local_sem, hssem, hrsem):
         at, core = place()
-        meet(torus_peers(at, core))
+        meet(torus_peers(at, core) + neighbours())
         partner = device(at, 1 - core)
         z, y, x = at["z"], at["y"], at["x"]
         local = pltpu.make_async_copy(own_ref.at[:, core], blocks.at[:, core, z, y, x, core], local_sem)
         local.start()
+        inner = pltpu.make_async_copy(x_ref, ext_ref.at[6:22, 8:40], hssem.at[8])
+        inner.start()
         pair = send(
             own_ref.at[:, 1 - core], blocks.at[:, 1 - core, z, y, x, core], psem.at[0, 0], psem.at[1, 0], partner
         )
@@ -104,6 +106,11 @@
         pair.wait_recv()
         sent = [pair]
         lasts = []
+        halos = []
+        for side, (row_step, col_step) in enumerate(SIDES):
+            src = x_ref.at[cut(OWN_ROWS, row_step), cut(OWN_COLS, col_step)]
+            dst = ext_ref.at[cut(HALO_ROWS, -row_step), cut(HALO_COLS, -col_step)]
+            halos.append(send(src, dst, hssem.at[side], hrsem.at[side], beside(row_step, col_step)))
         for stage in range(3):
             whole, rounds = {}, {}
             for part in range(3):
@@ -149,23 +156,34 @@
                 out_ref[pl.ds(first, 48), 128 * chunk : 128 * chunk + 128] = rows
 
         unpack(blocks, write)
+        for copy in halos:
+            copy.wait_recv()
+        for copy in halos:
+            copy.wait_send()
+        inner.wait()
 
     vmem = pl.BlockSpec(memory_space=pltpu.VMEM)
     return pl.pallas_call(
         kernel,
-        out_shape=(jax.ShapeDtypeStruct((768, 2304), BF), jax.ShapeDtypeStruct((768, 768), BF)),
-        in_specs=[vmem],
-        out_specs=(vmem, vmem),
+        out_shape=(
+            jax.ShapeDtypeStruct((768, 2304), BF),
+            jax.ShapeDtypeStruct((768, 768), BF),
+            jax.ShapeDtypeStruct((28, 48, 768), BF),
+        ),
+        in_specs=[vmem, vmem],
+        out_specs=(vmem, vmem, vmem),
         scratch_shapes=[
             pltpu.VMEM((3, 2, 4, 4, 4, 2, 3, 8, 128), BF),
             pltpu.SemaphoreType.DMA((3, 3, 4)),
             pltpu.SemaphoreType.DMA((3, 3, 4)),
             pltpu.SemaphoreType.DMA((2, 4)),
             pltpu.SemaphoreType.DMA,
+            pltpu.SemaphoreType.DMA((9,)),
+            pltpu.SemaphoreType.DMA((8,)),
         ],
         compiler_params=pltpu.CompilerParams(collective_id=0, has_side_effects=True),
         name="gather_weights",
-    )(own)
+    )(own, features)
 
 
 def to_blocks(qkv, out):
@@ -327,195 +345,213 @@
     )(first, second)
     return from_blocks(own)
 
-HEADS = 12
+
 RADIUS = 6
-QROWS = 16
-QCOLS = 16
-
-
-heads_together = 2
-
-
-def shifted(value, axis, steps):
-    count = lax.axis_size(axis)
-    pairs = [(source, (source + steps) % count) for source in range(count)]
-    return lax.ppermute(value, axis, pairs)
-
-
-def shifted_2(value, axis, steps):
-    count = lax.axis_size(axis)
-    leading, last = (max(0, -steps), min(count, count - steps))
-    return lax.ppermute(value, axis, [(source, source + steps) for source in range(leading, last)])
-
-
-def padded(array, sides, width, wrap):
-    for axis, dim in sides:
-        devices, length = (lax.axis_size(axis), array.shape[dim])
-        up = [(i, (i + 1) % devices) for i in range(devices if wrap else devices - 1)]
-        down = [(j, i) for i, j in up]
-        last = lax.slice_in_dim(array, length - width, length, axis=dim)
-        leading = lax.slice_in_dim(array, 0, width, axis=dim)
-        before = lax.ppermute(last, axis, up)
-        after = lax.ppermute(leading, axis, down)
-        array = jnp.concatenate([before, array, after], axis=dim)
-    return array
-
-
-def window_mask(row_first, query_rows, query_cols, key_rows, key_cols, radius, total_rows):
-    q_rows = row_first + jnp.arange(query_rows, dtype=jnp.int32)
-    k_rows = row_first - radius + jnp.arange(key_rows, dtype=jnp.int32)
-    row_start = jnp.clip(q_rows - radius, 0, total_rows - 2 * radius - 1)
-    row_valid = (k_rows[None, :] >= row_start[:, None]) & (
-        k_rows[None, :] <= row_start[:, None] + 2 * radius
+SIDES = ((-1, -1), (-1, 0), (-1, 1), (0, -1), (0, 1), (1, -1), (1, 0), (1, 1))
+OWN_ROWS = {-1: (0, 6), 0: (0, 16), 1: (10, 6)}
+OWN_COLS = {-1: (0, 8), 0: (0, 32), 1: (24, 8)}
+HALO_ROWS = {-1: (0, 6), 0: (6, 16), 1: (22, 6)}
+HALO_COLS = {-1: (0, 8), 0: (8, 32), 1: (40, 8)}
+
+
+def cut(table, step):
+    first, count = table[step]
+    return slice(first, first + count)
+
+
+def beside(row_step, col_step):
+    lat = (lax.axis_index("lat") + row_step + 8) % 8
+    lon = (lax.axis_index("lon") + col_step + 16) % 16
+    return (lat, lon)
+
+
+def neighbours():
+    return [beside(a, b) for a, b in SIDES]
+
+
+def window_bias(bias, start_of):
+    lat = lax.axis_index("lat")
+    shape = (32, 32, 128)
+
+    def body(i, carry):
+        group, part = i // 8, i % 8
+        key_row = lat * 16 + start_of(group) - 6 + part * 2 + lax.broadcasted_iota(jnp.int32, (2, 32, 128), 0)
+        key_col = lax.broadcasted_iota(jnp.int32, (2, 32, 128), 1)
+        lane = lax.broadcasted_iota(jnp.int32, (2, 32, 128), 2) & 63
+        query_row = lat * 16 + group * 4 + (lane >> 4)
+        first = jnp.clip(query_row - RADIUS, 0, 128 - 2 * RADIUS - 1)
+        apart = key_col - 8 - (lane & 15)
+        good = (key_row >= first) & (key_row <= first + 2 * RADIUS) & (apart >= -RADIUS) & (apart <= RADIUS)
+        bias[group, pl.ds(part * 64, 64)] = jnp.where(good, 0.0, -1e30).astype(F32).reshape(64, 128)
+        return carry
+
+    lax.fori_loop(0, 32, body, 0)
+
+
+def dot(a, b, left, right):
+    return lax.dot_general(a, b, (((left,), (right,)), ((), ())), preferred_element_type=F32)
+
+
+def spread(rows):
+    head = lax.broadcasted_iota(jnp.int32, (64, 256), 1) >> 6
+    return jnp.concatenate([jnp.where(head == h, rows, 0) for h in range(4)], axis=0)
+
+
+def gathered(full):
+    head = lax.broadcasted_iota(jnp.int32, (64, 256), 1) >> 6
+    out = full[0:64]
+    for h in range(1, 4):
+        out = jnp.where(head == h, full[64 * h : 64 * h + 64], out)
+    return out
+
+
+def attend(xext, grad_output, qkv_full, out_full):
+    def kernel(
+        x_ref, go_ref, wqkv_ref, wout_ref, att_ref, gp_ref, q, g, k, v, dk, dv, bias, out_s, out_c, out_r, in_s, in_c,
+        in_r, ssem, rsem,
+    ):
+        lat = lax.axis_index("lat")
+        low = jnp.where(lat == 0, 4, 0)
+        high = jnp.where(lat == 7, 8, 12)
+
+        def start_of(group):
+            return jnp.clip(group * 4, low, high)
+
+        meet(neighbours())
+        window_bias(bias, start_of)
+
+        def project_own(i, carry):
+            rows = x_ref[pl.ds(6 + 4 * i, 4), 8:40].reshape(128, 768)
+            grads = go_ref[pl.ds(4 * i, 4)].reshape(128, 768)
+            for t in range(3):
+                cols = slice(256 * t, 256 * t + 256)
+                head = dot(rows, wqkv_ref[:, cols], 1, 0).astype(BF).astype(F32) * 0.125
+                q[t, pl.ds(4 * i, 4)] = head.astype(BF).reshape(4, 32, 256)
+                head = dot(grads, wout_ref[cols, :], 1, 1).astype(BF)
+                g[t, pl.ds(4 * i, 4)] = head.reshape(4, 32, 256)
+            return carry
+
+        lax.fori_loop(0, 4, project_own, 0)
+
+        def project_all(i, carry):
+            rows = x_ref[pl.ds(4 * i, 4)].reshape(192, 768)
+            for t in range(3):
+                for ref, first in ((k, 768), (v, 1536)):
+                    cols = slice(first + 256 * t, first + 256 * t + 256)
+                    ref[t, pl.ds(4 * i, 4)] = dot(rows, wqkv_ref[:, cols], 1, 0).astype(BF).reshape(4, 48, 256)
+            for t in range(3):
+                dk[t, pl.ds(4 * i, 4)] = jnp.zeros((4, 48, 256), F32)
+                dv[t, pl.ds(4 * i, 4)] = jnp.zeros((4, 48, 256), F32)
+            return carry
+
+        lax.fori_loop(0, 7, project_all, 0)
+
+        def tile(i, carry):
+            t, group = i // 4, i % 4
+            start = start_of(group)
+            lanes = pl.ds(pl.multiple_of(t * 256, 256), 256)
+            mask = bias[group]
+            mask = jnp.concatenate([mask, mask], axis=1)
+            for j in range(2):
+                q_cols, k_cols = slice(16 * j, 16 * j + 16), slice(16 * j, 16 * j + 32)
+                q_b = spread(q[t, pl.ds(4 * group, 4), q_cols].reshape(64, 256))
+                g_b = spread(g[t, pl.ds(4 * group, 4), q_cols].reshape(64, 256))
+                k4 = k[t, pl.ds(start, 16), k_cols].reshape(512, 256)
+                v4 = v[t, pl.ds(start, 16), k_cols].reshape(512, 256)
+                scores = dot(k4, q_b, 1, 1) + mask
+                top = jnp.max(scores, axis=0, keepdims=True)
+                terms = jnp.exp(scores - top)
+                probs = terms * (1.0 / jnp.sum(terms, axis=0, keepdims=True))
+                probs_b = probs.astype(BF)
+                att = gathered(dot(probs_b, v4, 0, 0)).astype(BF)
+                att_ref[pl.ds(4 * group, 4), q_cols, lanes] = att.reshape(4, 16, 256)
+                dprob = dot(v4, g_b, 1, 1)
+                row_term = jnp.sum(probs * dprob, axis=0, keepdims=True)
+                dscore = (probs * (dprob - row_term)).astype(BF)
+                dq = gathered(dot(dscore, k4, 0, 0)) * 0.125
+                gp_ref[pl.ds(4 * group, 4), q_cols, lanes] = dq.astype(BF).reshape(4, 16, 256)
+                dk[t, pl.ds(start, 16), k_cols] += dot(dscore, q_b, 1, 0).reshape(16, 32, 256)
+                dv[t, pl.ds(start, 16), k_cols] += dot(probs_b, g_b, 1, 0).reshape(16, 32, 256)
+            return carry
+
+        lax.fori_loop(0, 12, tile, 0)
+
+        def slot(side, out):
+            row_step, col_step = SIDES[side]
+            if row_step == 0:
+                return (out_s if out else in_s).at[0 if col_step < 0 else 1]
+            if col_step == 0:
+                return (out_r if out else in_r).at[0 if row_step < 0 else 1]
+            return (out_c if out else in_c).at[(0 if row_step < 0 else 2) + (0 if col_step < 0 else 1)]
+
+        copies = []
+        for side, (row_step, col_step) in enumerate(SIDES):
+            rows, cols = cut(HALO_ROWS, row_step), cut(HALO_COLS, col_step)
+            for t in range(3):
+                for which, ref in ((0, dk), (1, dv)):
+                    slot(side, True)[which, t] = ref[t, rows, cols].astype(BF)
+            copies.append(send(slot(side, True), slot(7 - side, False), ssem.at[side], rsem.at[side], beside(row_step, col_step)))
+        for side, (row_step, col_step) in enumerate(SIDES):
+            copies[side].wait_recv()
+            r0, nr = OWN_ROWS[-row_step]
+            c0, nc = OWN_COLS[-col_step]
+            for t in range(3):
+                for which, ref in ((0, dk), (1, dv)):
+                    ref[t, 6 + r0 : 6 + r0 + nr, 8 + c0 : 8 + c0 + nc] += slot(7 - side, False)[which, t].astype(F32)
+        for t in range(3):
+            for first, ref in ((768, dk), (1536, dv)):
+                gp_ref[:, :, first + 256 * t : first + 256 * t + 256] = ref[t, 6:22, 8:40].astype(BF)
+        for copy in copies:
+            copy.wait_send()
+
+    vmem = pl.BlockSpec(memory_space=pltpu.VMEM)
+    return pl.pallas_call(
+        kernel,
+        out_shape=(jax.ShapeDtypeStruct((16, 32, 768), BF), jax.ShapeDtypeStruct((16, 32, 2304), BF)),
+        in_specs=[vmem] * 4,
+        out_specs=(vmem, vmem),
+        scratch_shapes=[
+            pltpu.VMEM((3, 16, 32, 256), BF),
+            pltpu.VMEM((3, 16, 32, 256), BF),
+            pltpu.VMEM((3, 28, 48, 256), BF),
+            pltpu.VMEM((3, 28, 48, 256), BF),
+            pltpu.VMEM((3, 28, 48, 256), F32),
+            pltpu.VMEM((3, 28, 48, 256), F32),
+            pltpu.VMEM((4, 512, 128), F32),
+            pltpu.VMEM((2, 2, 3, 16, 8, 256), BF),
+            pltpu.VMEM((4, 2, 3, 6, 8, 256), BF),
+            pltpu.VMEM((2, 2, 3, 6, 32, 256), BF),
+            pltpu.VMEM((2, 2, 3, 16, 8, 256), BF),
+            pltpu.VMEM((4, 2, 3, 6, 8, 256), BF),
+            pltpu.VMEM((2, 2, 3, 6, 32, 256), BF),
+            pltpu.SemaphoreType.DMA((8,)),
+            pltpu.SemaphoreType.DMA((8,)),
+        ],
+        compiler_params=pltpu.CompilerParams(collective_id=2, has_side_effects=True, vmem_limit_bytes=60 << 20),
+        name="attend",
+    )(xext, grad_output, qkv_full, out_full)
+
+
+def shards(features, grad_output, qkv_weight, out_weight):
+    qkv_full, out_full, xext = gather(to_blocks(qkv_weight, out_weight), features)
+    attended, grad_proj = attend(xext, grad_output, qkv_full, out_full)
+    x_rows = features.reshape(-1, 768)
+    grad_rows = grad_output.reshape(-1, 768)
+    grad_proj = grad_proj.reshape(-1, 2304)
+    grad_features = lax.dot_general(
+        grad_proj, qkv_full, (((1,), (1,)), ((), ())), preferred_element_type=F32
     )
-    q_cols = jnp.arange(query_cols, dtype=jnp.int32)
-    k_cols = jnp.arange(key_cols, dtype=jnp.int32)
-    col_valid = (k_cols[None, :] >= q_cols[:, None]) & (
-        k_cols[None, :] <= q_cols[:, None] + 2 * radius
-    )
-    allowed = row_valid[:, None, :, None] & col_valid[None, :, None, :]
-    return allowed.reshape(query_rows * query_cols, key_rows * key_cols)
-
-
-def tile_terms(queries, keys, values, grad_heads, window, head_count, head_dim):
-    q_count = queries.shape[0]
-    k_count = keys.shape[0]
-    softmax_scale = 1.0 / math.sqrt(head_dim)
-    query_h = queries.reshape(q_count, head_count, head_dim)
-    key_h = keys.reshape(k_count, head_count, head_dim)
-    value_h = values.reshape(k_count, head_count, head_dim)
-    grad_h = grad_heads.reshape(q_count, head_count, head_dim)
-    scores = (
-        jnp.einsum("qhe,khe->hqk", query_h, key_h, preferred_element_type=jnp.float32)
-        * softmax_scale
-    )
-    scores = jnp.where(window[None], scores, -jnp.inf)
-    row_max = jnp.max(scores, axis=2, keepdims=True)
-    exp_terms = jnp.exp(scores - row_max)
-    prob_f32 = exp_terms / jnp.sum(exp_terms, axis=2, keepdims=True)
-    prob_b16 = prob_f32.astype(jnp.bfloat16)
-    attended = jnp.einsum(
-        "hqk,khe->qhe", prob_b16, value_h, preferred_element_type=jnp.float32
-    ).astype(jnp.bfloat16)
-    row_term = jnp.sum(grad_h.astype(jnp.float32) * attended.astype(jnp.float32), axis=2)
-    dprob = jnp.einsum("qhe,khe->hqk", grad_h, value_h, preferred_element_type=jnp.float32)
-    dscore = (prob_f32 * (dprob - row_term.T[:, :, None])).astype(jnp.bfloat16)
-    grad_query = jnp.einsum("hqk,khe->qhe", dscore, key_h, preferred_element_type=jnp.float32)
-    grad_key = jnp.einsum("hqk,qhe->khe", dscore, query_h, preferred_element_type=jnp.float32)
-    grad_value = jnp.einsum("hqk,qhe->khe", prob_b16, grad_h, preferred_element_type=jnp.float32)
-    model_part = head_count * head_dim
-    return (
-        attended.reshape(q_count, model_part),
-        grad_query.reshape(q_count, model_part),
-        grad_key.reshape(k_count, model_part),
-        grad_value.reshape(k_count, model_part),
-    )
-
-
-def turn_lon(strip_part, offset):
-    return shifted(strip_part.astype(jnp.bfloat16), "lon", offset).astype(strip_part.dtype)
-
-
-def turn_lat(strip_part, offset):
-    return shifted_2(strip_part.astype(jnp.bfloat16), "lat", offset).astype(strip_part.dtype)
-
-
-def shards(features, grad_output, qkv_weight, out_weight):
-    lat_rows, lon_cols, model_width = features.shape
-    radius = RADIUS
-    head_dim = model_width // HEADS
-    qkv_full, out_full = gather(to_blocks(qkv_weight, out_weight))
-    x_rows = features.reshape(-1, model_width)
-    grad_rows = grad_output.reshape(-1, model_width)
-    projected = jnp.dot(x_rows, qkv_full, preferred_element_type=jnp.float32).astype(jnp.bfloat16)
-    projected = projected.reshape(lat_rows, lon_cols, 3 * model_width)
-    grad_attn = lax.dot_general(
-        grad_rows, out_full, (((1,), (1,)), ((), ())), preferred_element_type=jnp.float32
-    )
-    grad_attn = grad_attn.astype(jnp.bfloat16).reshape(lat_rows, lon_cols, model_width)
-    queries = projected[..., :model_width]
-    key_value = projected[..., model_width:]
-    lon_wide = padded(key_value, (("lon", 1),), radius, True)
-    extended = padded(lon_wide, (("lat", 0),), radius, False)
-    total_rows = lat_rows * lax.axis_size("lat")
-    lat_first = lax.axis_index("lat") * lat_rows
-    key_rows = QROWS + 2 * radius
-    key_cols = QCOLS + 2 * radius
-    wide_cols = lon_cols + 2 * radius
-    grad_kv = jnp.zeros((lat_rows + 2 * radius, wide_cols, 2 * model_width), jnp.float32)
-    window = window_mask(lat_first + 0, QROWS, QCOLS, key_rows, key_cols, radius, total_rows)
-    out_row = []
-    query_row = []
-    for col_index in range(lon_cols // QCOLS):
-        left_col = col_index * QCOLS
-        q_tile = queries[0:QROWS, left_col : left_col + QCOLS].reshape(-1, model_width)
-        g_tile = grad_attn[0:QROWS, left_col : left_col + QCOLS].reshape(-1, model_width)
-        kv_tile = extended[0:key_rows, left_col : left_col + key_cols].reshape(-1, 2 * model_width)
-        out_parts, query_parts, key_parts, value_parts = ([], [], [], [])
-        for first_head in range(0, HEADS, heads_together):
-            col_low = first_head * head_dim
-            col_high = col_low + heads_together * head_dim
-            attended, grad_query, grad_key, grad_value = tile_terms(
-                q_tile[:, col_low:col_high],
-                kv_tile[:, col_low:col_high],
-                kv_tile[:, model_width + col_low : model_width + col_high],
-                g_tile[:, col_low:col_high],
-                window,
-                heads_together,
-                head_dim,
-            )
-            out_parts.append(attended)
-            query_parts.append(grad_query)
-            key_parts.append(grad_key)
-            value_parts.append(grad_value)
-        out_row.append(jnp.concatenate(out_parts, axis=1).reshape(QROWS, QCOLS, model_width))
-        query_row.append(jnp.concatenate(query_parts, axis=1).reshape(QROWS, QCOLS, model_width))
-        key_part = jnp.concatenate(key_parts + value_parts, axis=1).reshape(
-            key_rows, key_cols, 2 * model_width
-        )
-        grad_kv = grad_kv.at[0:key_rows, left_col : left_col + key_cols].add(key_part)
-    out_blocks = jnp.concatenate(out_row, axis=1)
-    query_blocks = jnp.concatenate(query_row, axis=1)
-    from_right = turn_lon(grad_kv[:, :radius], -1)
-    from_left = turn_lon(grad_kv[:, wide_cols - radius :], 1)
-    middle = grad_kv[:, radius : radius + lon_cols]
-    middle = middle.at[:, :radius].add(from_left)
-    middle = middle.at[:, lon_cols - radius :].add(from_right)
-    from_below = turn_lat(middle[:radius], -1)
-    from_above = turn_lat(middle[lat_rows + radius :], 1)
-    interior = middle[radius : radius + lat_rows]
-    interior = interior.at[:radius].add(from_above)
-    interior = interior.at[lat_rows - radius :].add(from_below)
-    softmax_scale = 1.0 / math.sqrt(head_dim)
-    query_all = query_blocks.reshape(-1, model_width)
-    grad_query = (query_all * softmax_scale).astype(jnp.bfloat16)
-    grad_key = (
-        (interior[..., :model_width] * softmax_scale).astype(jnp.bfloat16).reshape(-1, model_width)
-    )
-    grad_value = interior[..., model_width:].astype(jnp.bfloat16).reshape(-1, model_width)
-    grad_proj = jnp.concatenate([grad_query, grad_key, grad_value], axis=1)
-    attended_rows = out_blocks.reshape(-1, model_width)
-    grad_features = lax.dot_general(
-        grad_proj, qkv_full, (((1,), (1,)), ((), ())), preferred_element_type=jnp.float32
-    )
-    grad_features = grad_features.astype(jnp.bfloat16).reshape(lat_rows, lon_cols, model_width)
-    first_term = lax.dot_general(
-        x_rows, grad_proj, (((0,), (0,)), ((), ())), preferred_element_type=jnp.float32
-    )
+    grad_features = grad_features.astype(BF).reshape(16, 32, 768)
+    first_term = lax.dot_general(x_rows, grad_proj, (((0,), (0,)), ((), ())), preferred_element_type=F32)
     second_term = lax.dot_general(
-        attended_rows, grad_rows, (((0,), (0,)), ((), ())), preferred_element_type=jnp.float32
+        attended.reshape(-1, 768), grad_rows, (((0,), (0,)), ((), ())), preferred_element_type=F32
     )
     my_grads = scatter(first_term, second_term)
-    return (grad_features, my_grads[:, : 3 * model_width], my_grads[:, 3 * model_width :])
+    return (grad_features, my_grads[:, :2304], my_grads[:, 2304:])
 
 
 def solution(mesh):
-    placed = (
-        P("lat", "lon", None),
-        P("lat", "lon", None),
-        P(("lat", "lon"), None),
-        P(("lat", "lon"), None),
-    )
+    placed = (P("lat", "lon", None), P("lat", "lon", None), P(("lat", "lon"), None), P(("lat", "lon"), None))
     return jax.shard_map(
         shards,
         mesh=mesh,

time: 495 us -> 205 us (0.41)
  local copies, waits for them, and re-layouts: 218 us -> 2.8 us
  matrix products: 110 us -> 12 us
  Pallas kernels: 90.8 us -> 188 us
  waiting for transfers between devices: 28.8 us -> 0 us
  other arithmetic: 28.5 us -> 0.8 us
  starting transfers between devices: 10.7 us -> 0 us
    pallas_call x0 -> x1, Pallas kernels: none -> 82.7 us  [attend(): pl.pallas_call(kernel, out_shape=(jax.ShapeDtypeStruct((16, 32, 768), BF)...]
    unnamed x348 -> x10, local copies, waits for them, and re-layouts: 77 us -> 0.02 us
    dot_general x63 -> x1, matrix products: 63.9 us -> 2.28 us  [shards(): lax.dot_general(attended.reshape(-1, 768), grad_rows, (((0,), (0,)), ((),...]
    concatenate x54 -> x0, local copies, waits for them, and re-layouts: 44.4 us -> none  [the longest x26 27.2 us: shards(): jnp.concatenate(key_parts + value_parts, axis=1)]
    transpose x36 -> x0, local copies, waits for them, and re-layouts: 42.4 us -> none  [the longest x12 20 us: tile_terms(): jnp.einsum('hqk,qhe->khe', dscore, query_h, preferred_element_type=jnp.fl...]
    sub x12 -> x0, matrix products: 37.9 us -> none  [tile_terms(): exp_terms = jnp.exp(scores - row_max)]
    ppermute x8 -> x0, waiting for transfers between devices: 28.8 us -> none  [the longest x2 15.9 us: shifted_2(): lax.ppermute(value, axis, [(source, source + steps) for source in range(l...]
    pallas_call x1, Pallas kernels: 41 us -> 63.1 us  [gather(): pl.pallas_call(kernel, out_shape=(jax.ShapeDtypeStruct((768, 2304), BF),...]
  transfers between devices with their start and end apart: 8 -> 0, of which waited for: 5 -> 0; matrix products, arithmetic and copies ran while one was open for 13% -> 0% of each run, Pallas kernels for 0% -> 0%
where the time goes in v2:
time: 205 us; the launch traced here: 204 us
  Pallas kernels  188 us (92%)
  matrix products  12 us (6%)
  local copies, waits for them, and re-layouts  2.8 us (1%)
    pallas_call x1, Pallas kernels, attend(): pl.pallas_call(kernel, out_shape=(jax.ShapeDtypeStruct((16, 32, 768), BF)...  82.7 us
    pallas_call x1, Pallas kernels, gather(): pl.pallas_call(kernel, out_shape=(jax.ShapeDtypeStruct((768, 2304), BF),...  63.1 us
    pallas_call x1, Pallas kernels, scatter(): pl.pallas_call(kernel, out_shape=jax.ShapeDtypeStruct((3, 2) + tail, F32)...  42.3 us
    dot_general x1, matrix products, shards(): lax.dot_general(x_rows, grad_proj, (((0,), (0,)), ((), ())), preferred_el...  4.97 us
    dot_general x1, matrix products, shards(): lax.dot_general(grad_proj, qkv_full, (((1,), (1,)), ((), ())), preferred_...  4.71 us

profile of v2, /device:TPU:1, one launch (start us, length us, event | category | flops | bytes accessed | tf_op | source)
XLA Modules:
  0.0 204.3 jit_solution(15116804305247689249)
XLA Ops:
  0.6 0.8 pad_maximum_fusion
  1.4 0.6 reshape.28.own_ref
  2.1 63.1 %gather_weights.1 = (bf16[768,2304]{1,0:T(8,128)(2,1)}, bf16[768,768]{1,0:T(8,128)(2,1)}, bf16[28,48,768]{2,1,0:T(8,128)(2,1)}) custom-call(bf16[3,2,3,8,128]{4,3,2,1,0:T(8,128)(2,1)} %reshape.28.own_ref, bf16[16,32,768]{2,1,0:T(8,128)(2,1)} %x_ref.1), custom_call_target="tpu_custom_call" | custom-call | tf_op jit(solution)/shard_map/gather_weights/pallas_call | solution.py:166
  65.2 0.0 copy-start
  65.2 82.7 %attend.1 = (bf16[16,32,768]{2,1,0:T(8,128)(2,1)}, bf16[16,32,2304]{2,1,0:T(8,128)(2,1)}) custom-call(bf16[28,48,768]{2,1,0:T(8,128)(2,1)} %get-tuple-element.8.x_ref, bf16[16,32,768]{2,1,0:T(8,128)(2,1)} %go_ref.1, bf16[768,2304]{1,0:T(8,128)(2,1)} %get-tuple-element.9.wqkv_ref, bf16[768,768]{1,0:T(8,128)(2,1)} %get-tuple-element.10.wout_ref), custom_call_target="tpu_custom_call" | custom-call | tf_op jit(solution)/shard_map/attend/pallas_call | solution.py:508
  147.9 0.0 copy-done
  147.9 0.0 copy-start.1
  147.9 0.0 copy-start.2
  148.0 4.7 %convolution_convert_fusion = bf16[512,768]{1,0:T(8,128)(2,1)} fusion(bf16[512,2304]{1,0:T(8,128)(2,1)} %bitcast.22, bf16[768,2304]{1,0:T(8,128)(2,1)S(1)} %copy-done), kind=kOutput, calls=%fused_computation.2 | convolution fusion | flops 1812332544 | bytes 6684672 | tf_op jit(solution)/shard_map/dot_general | solution.py:541
  152.7 0.0 copy-done.1
  152.7 0.0 copy-done.2
  152.7 0.0 copy-start.3
  152.7 0.0 copy-start.4
  152.7 5.0 %convolution_bitcast_fusion.qkv_ref = f32[768,2304]{1,0:T(8,128)} fusion(bf16[16,32,2304]{2,1,0:T(8,128)(2,1)S(1)} %copy-done.2, bf16[16,32,768]{2,1,0:T(8,128)(2,1)S(1)} %copy-done.1), kind=kOutput, calls=%fused_computation | convolution fusion | flops 1811939328 | bytes 10223616 | tf_op jit(solution)/shard_map/dot_general | solution.py:545
  157.7 0.0 copy-done.3
  157.7 0.0 copy-done.4
  157.7 2.3 %convolution_bitcast_fusion.1.out_ref = f32[768,768]{1,0:T(8,128)} fusion(bf16[16,32,768]{2,1,0:T(8,128)(2,1)S(1)} %copy-done.4, bf16[16,32,768]{2,1,0:T(8,128)(2,1)S(1)} %copy-done.3), kind=kOutput, calls=%fused_computation.1 | convolution fusion | flops 603979776 | bytes 3932160 | tf_op jit(solution)/shard_map/dot_general | solution.py:546
  159.9 42.3 %scatter_grads.1 = f32[3,2,3,8,128]{4,3,2,1,0:T(8,128)} custom-call(f32[768,2304]{1,0:T(8,128)} %convolution_bitcast_fusion.qkv_ref, f32[768,768]{1,0:T(8,128)} %convolution_bitcast_fusion.1.out_ref), custom_call_target="tpu_custom_call" | custom-call | tf_op jit(solution)/shard_map/scatter_grads/pallas_call | solution.py:323
  202.2 0.9 reshape.31
  203.1 0.6 slice.8
  203.7 0.6 slice.9
Async XLA Ops:
  65.2 82.7 %copy-start = (bf16[768,2304]{1,0:T(8,128)(2,1)S(1)}, bf16[768,2304]{1,0:T(8,128)(2,1)}, u32[]{:S(2)}) copy-start(bf16[768,2304]{1,0:T(8,128)(2,1)} %get-tuple-element.9.wqkv_ref) | copy-start | bytes 10616836
  147.9 4.7 %copy-start.1 = (bf16[16,32,768]{2,1,0:T(8,128)(2,1)S(1)}, bf16[16,32,768]{2,1,0:T(8,128)(2,1)}, u32[]{:S(2)}) copy-start(bf16[16,32,768]{2,1,0:T(8,128)(2,1)} %x_ref.1) | copy-start | bytes 2359300
  147.9 4.7 %copy-start.2 = (bf16[16,32,2304]{2,1,0:T(8,128)(2,1)S(1)}, bf16[16,32,2304]{2,1,0:T(8,128)(2,1)}, u32[]{:S(2)}) copy-start(bf16[16,32,2304]{2,1,0:T(8,128)(2,1)} %get-tuple-element.11) | copy-start | bytes 7077892
  152.7 5.0 %copy-start.3 = (bf16[16,32,768]{2,1,0:T(8,128)(2,1)S(1)}, bf16[16,32,768]{2,1,0:T(8,128)(2,1)}, u32[]{:S(2)}) copy-start(bf16[16,32,768]{2,1,0:T(8,128)(2,1)} %go_ref.1) | copy-start | bytes 2359300
  152.7 5.0 %copy-start.4 = (bf16[16,32,768]{2,1,0:T(8,128)(2,1)S(1)}, bf16[16,32,768]{2,1,0:T(8,128)(2,1)}, u32[]{:S(2)}) copy-start(bf16[16,32,768]{2,1,0:T(8,128)(2,1)} %get-tuple-element.12) | copy-start | bytes 2359300

commit v3 on v2

v3 whole, which is shorter than its diff:
```python
import jax
import jax.numpy as jnp
from jax import lax
from jax.experimental import pallas as pl
from jax.experimental.pallas import tpu as pltpu
from jax.sharding import PartitionSpec as P

MESH = pl.DeviceIdType.MESH
BF = jnp.bfloat16
F32 = jnp.float32


def place():
    lat = lax.axis_index("lat")
    lon = lax.axis_index("lon")
    z, x_lo = lat // 2, lat % 2
    y, x_hi, core = lon // 4, (lon // 2) % 2, lon % 2
    return {"z": z, "y": y, "x": x_hi * 2 + x_lo}, core


def device(at, core):
    return (at["z"] * 2 + at["x"] % 2, at["y"] * 4 + (at["x"] // 2) * 2 + core)


def moved(at, axis, steps):
    out = dict(at)
    out[axis] = (at[axis] + steps + 4) % 4
    return out


def meet(peers):
    barrier = pltpu.get_barrier_semaphore()
    for peer in peers:
        pl.semaphore_signal(barrier, inc=1, device_id=peer, device_id_type=MESH)
    pl.semaphore_wait(barrier, len(peers))


def torus_peers(at, core):
    peers = [device(at, 1 - core)]
    for axis in ("z", "y", "x"):
        for steps in (1, 2, 3):
            peers.append(device(moved(at, axis, steps), core))
    return peers


def region(at, full, axis=None, coord=None):
    index = []
    for name in ("z", "y", "x"):
        if name == axis:
            index.append(coord)
        elif name in full:
            index.append(slice(None))
        else:
            index.append(at[name])
    return tuple(index)


def send(src, dst, ssem, rsem, peer):
    copy = pltpu.make_async_remote_copy(
        src_ref=src, dst_ref=dst, send_sem=ssem, recv_sem=rsem, device_id=peer, device_id_type=MESH
    )
    copy.start()
    return copy


def unpack(blocks, write):
    def body(step, carry):
        z, rest = step // 4, step % 4
        x_lo, y_pair = rest // 2, rest % 2
        for unit in range(6):
            pieces = []
            for y in range(2):
                for x_hi in range(2):
                    for core in range(2):
                        piece = blocks[core, unit, z, 2 * y_pair + y, 2 * x_hi + x_lo]
                        pieces.append(piece.astype(F32).reshape(24, 128))
            for chunk in range(4):
                rows = jnp.concatenate([p[6 * chunk : 6 * chunk + 6] for p in pieces], axis=0)
                write(step, 4 * unit + chunk, rows.astype(BF))
        return carry

    lax.fori_loop(0, 16, body, 0)


GATHER_PARTS = ((0, 4, "z", "y"), (4, 2, "y", "z"))


def gather(own, features):
    def kernel(
        own_ref, x_ref, qkv_ref, out_ref, ext_ref, blocks, sem1, sem2, sem3, psem, local_sem, hssem, hrsem
    ):
        at, core = place()
        z, y, x = at["z"], at["y"], at["x"]
        local = pltpu.make_async_copy(own_ref, blocks.at[core, :, z, y, x], local_sem.at[0])
        local.start()
        inner = pltpu.make_async_copy(x_ref, ext_ref.at[6:22, 8:40], local_sem.at[1])
        inner.start()
        meet(torus_peers(at, core) + neighbours())
        partner = device(at, 1 - core)
        sent = []
        first = []
        for k in range(3):
            first.append(
                send(
                    own_ref, blocks.at[core, :, z, y, x], sem1.at[0, k], sem1.at[1, k],
                    device(moved(at, "x", k + 1), core),
                )
            )
        halos = []
        for side, (row_step, col_step) in enumerate(SIDES):
            src = x_ref.at[cut(OWN_ROWS, row_step), cut(OWN_COLS, col_step)]
            dst = ext_ref.at[cut(HALO_ROWS, -row_step), cut(HALO_COLS, -col_step)]
            halos.append(send(src, dst, hssem.at[side], hrsem.at[side], beside(row_step, col_step)))
        local.wait()
        for copy in first:
            copy.wait_recv()
        second = {}
        for part, (unit, count, axis, _) in enumerate(GATHER_PARTS):
            where = (core, slice(unit, unit + count)) + region(at, "x")
            for k in range(3):
                second[part, k] = send(
                    blocks.at[where], blocks.at[where], sem2.at[0, part, k], sem2.at[1, part, k],
                    device(moved(at, axis, k + 1), core),
                )
        third, passed = {}, []

        def hand(part, k, where):
            passed.append(
                send(blocks.at[where], blocks.at[where], psem.at[0, part, k], psem.at[1, part, k], partner)
            )

        for part, (unit, count, axis, last) in enumerate(GATHER_PARTS):
            for k in range(3):
                second[part, k].wait_recv()
            where = (core, slice(unit, unit + count)) + region(at, ("x", axis), last, at[last])
            for k, steps in ((0, 1), (1, -1)):
                third[part, k] = send(
                    blocks.at[where], blocks.at[where], sem3.at[0, part, k], sem3.at[1, part, k],
                    device(moved(at, last, steps), core),
                )
            hand(part, 0, where)
        for part, (unit, count, axis, last) in enumerate(GATHER_PARTS):
            for k, steps in ((0, 1), (1, -1)):
                third[part, k].wait_recv()
                back = region(at, ("x", axis), last, (at[last] - steps + 4) % 4)
                half = count // 2
                where = (core, slice(unit + k * half, unit + k * half + half)) + back
                third[part, 2 + k] = send(
                    blocks.at[where], blocks.at[where], sem3.at[0, part, 2 + k], sem3.at[1, part, 2 + k],
                    device(moved(at, last, steps), core),
                )
                hand(part, 1 + k, (core, slice(unit, unit + count)) + back)
        for part, (unit, count, axis, last) in enumerate(GATHER_PARTS):
            half = count // 2
            far = region(at, ("x", axis), last, (at[last] + 2) % 4)
            for k in range(2):
                third[part, 2 + k].wait_recv()
                hand(part, 3 + k, (core, slice(unit + k * half, unit + k * half + half)) + far)
        for copy in passed:
            copy.wait_recv()

        def write(step, chunk, rows):
            first_row = pl.multiple_of(step * 48, 16)
            if chunk < 18:
                qkv_ref[pl.ds(first_row, 48), 128 * chunk : 128 * chunk + 128] = rows
            else:
                chunk -= 18
                out_ref[pl.ds(first_row, 48), 128 * chunk : 128 * chunk + 128] = rows

        unpack(blocks, write)
        for copy in halos:
            copy.wait_recv()
        for copy in halos + first + list(second.values()) + list(third.values()) + passed:
            copy.wait_send()
        inner.wait()

    vmem = pl.BlockSpec(memory_space=pltpu.VMEM)
    return pl.pallas_call(
        kernel,
        out_shape=(
            jax.ShapeDtypeStruct((768, 2304), BF),
            jax.ShapeDtypeStruct((768, 768), BF),
            jax.ShapeDtypeStruct((28, 48, 768), BF),
        ),
        in_specs=[vmem, vmem],
        out_specs=(vmem, vmem, vmem),
        scratch_shapes=[
            pltpu.VMEM((2, 6, 4, 4, 4, 3, 8, 128), BF),
            pltpu.SemaphoreType.DMA((2, 3)),
            pltpu.SemaphoreType.DMA((2, 2, 3)),
            pltpu.SemaphoreType.DMA((2, 2, 4)),
            pltpu.SemaphoreType.DMA((2, 2, 5)),
            pltpu.SemaphoreType.DMA((2,)),
            pltpu.SemaphoreType.DMA((8,)),
            pltpu.SemaphoreType.DMA((8,)),
        ],
        compiler_params=pltpu.CompilerParams(collective_id=0, has_side_effects=True),
        name="gather_weights",
    )(own, features)


def to_blocks(qkv, out):
    rows = jnp.concatenate([qkv, out], axis=1)
    rows = rows.reshape(6, 6, 4, 128).transpose(1, 2, 0, 3)
    return rows.reshape(6, 3, 8, 128)


def from_blocks(blocks):
    rows = blocks.reshape(6, 4, 6, 128).transpose(2, 0, 1, 3)
    return rows.reshape(6, 3072)


SCATTER_ORDERS = (("z", "y", "x"), ("x", "z", "y"), ("y", "x", "z"))


def scatter(first, second):
    def kernel(
        qkv_ref, out_ref, own_ref, blocks, pair_in, half_in, whole_in, mid_in, last_in, psem, ssem, msem, lsem
    ):
        at, core = place()
        meet(torus_peers(at, core))
        partner = device(at, 1 - core)

        def pack(part):
            def body(step, carry):
                z, rest = step // 4, step % 4
                x_lo, y_pair = rest // 2, rest % 2
                first_row = pl.multiple_of(step * 48, 16)
                for unit in (2 * part, 2 * part + 1):
                    chunks = []
                    for q in range(4):
                        c = 4 * unit + q
                        ref, c = (qkv_ref, c) if c < 18 else (out_ref, c - 18)
                        chunks.append(ref[pl.ds(first_row, 48), 128 * c : 128 * c + 128])
                    for e in range(8):
                        y, x_hi, to = e // 4, (e // 2) % 2, e % 2
                        rows = jnp.concatenate([c[6 * e : 6 * e + 6] for c in chunks], axis=0)
                        blocks[to, unit, z, 2 * y_pair + y, 2 * x_hi + x_lo] = rows.reshape(3, 8, 128).astype(BF)
                return carry

            lax.fori_loop(0, 16, body, 0)

        def each(count, body):
            lax.fori_loop(0, count, lambda i, c: (body(i), c)[1], 0)

        def spot(unit, where, inner):
            inner = list(inner)
            return (core, unit) + tuple(inner.pop(0) if isinstance(w, slice) else w for w in where)

        pairs, early, late, mid, last = [], {}, {}, {}, {}
        for part in range(3):
            pack(part)
            units = slice(2 * part, 2 * part + 2)
            pairs.append(
                send(blocks.at[1 - core, units], pair_in.at[units], psem.at[0, part], psem.at[1, part], partner)
            )
        for part, (a0, a1, a2) in enumerate(SCATTER_ORDERS):
            pairs[part].wait_recv()

            def add(i, part=part):
                unit, z, y = 2 * part + i // 16, (i // 4) % 4, i % 4
                total = blocks[core, unit, z, y].astype(F32) + pair_in[unit, z, y].astype(F32)
                blocks[core, unit, z, y] = total.astype(BF)

            each(32, add)
            far = region(at, (a1, a2), a0, (at[a0] + 2) % 4)
            for k, steps in ((0, 1), (1, -1)):
                early[part, k] = send(
                    blocks.at[(core, 2 * part + k) + far], half_in.at[part, k], ssem.at[0, part, k],
                    ssem.at[1, part, k], device(moved(at, a0, steps), core),
                )
        for part, (a0, a1, a2) in enumerate(SCATTER_ORDERS):
            for k, steps in ((0, 1), (1, -1)):
                early[part, k].wait_recv()
                near = region(at, (a1, a2), a0, (at[a0] + steps + 4) % 4)

                def add(i, part=part, k=k, near=near):
                    here = spot(2 * part + k, near, (i // 4, i % 4))
                    total = blocks[here].astype(F32) + half_in[part, k, i // 4, i % 4].astype(F32)
                    blocks[here] = total.astype(BF)

                each(16, add)
                late[part, k] = send(
                    blocks.at[(core, slice(2 * part, 2 * part + 2)) + near], whole_in.at[part, k],
                    ssem.at[0, part, 2 + k], ssem.at[1, part, 2 + k], device(moved(at, a0, steps), core),
                )
        for part, (a0, a1, a2) in enumerate(SCATTER_ORDERS):
            late[part, 0].wait_recv()
            late[part, 1].wait_recv()
            mine = region(at, (a1, a2), a0, at[a0])

            def add(i, part=part, mine=mine):
                j, p, q = i // 16, (i // 4) % 4, i % 4
                here = spot(2 * part + j, mine, (p, q))
                total = blocks[here].astype(F32) + whole_in[part, 0, j, p, q].astype(F32)
                blocks[here] = (total + whole_in[part, 1, j, p, q].astype(F32)).astype(BF)

            each(32, add)
            for k in range(3):
                where = region(at, (a2,), a1, (at[a1] + k + 1) % 4)
                mid[part, k] = send(
                    blocks.at[(core, slice(2 * part, 2 * part + 2)) + where], mid_in.at[part, k],
                    msem.at[0, part, k], msem.at[1, part, k], device(moved(at, a1, k + 1), core),
                )
        for part, (a0, a1, a2) in enumerate(SCATTER_ORDERS):
            for k in range(3):
                mid[part, k].wait_recv()
            mine = region(at, (a2,), a1, at[a1])
            for i in range(8):
                j, p = i // 4, i % 4
                here = spot(2 * part + j, mine, (p,))
                total = blocks[here].astype(F32)
                for k in range(3):
                    total = total + mid_in[part, k, j, p].astype(F32)
                blocks[here] = total.astype(BF)
            for k in range(3):
                where = region(at, (), a2, (at[a2] + k + 1) % 4)
                last[part, k] = send(
                    blocks.at[(core, slice(2 * part, 2 * part + 2)) + where], last_in.at[part, k],
                    lsem.at[0, part, k], lsem.at[1, part, k], device(moved(at, a2, k + 1), core),
                )
        for part in range(3):
            for k in range(3):
                last[part, k].wait_recv()
            for j in range(2):
                total = blocks[(core, 2 * part + j) + region(at, ())].astype(F32)
                for k in range(3):
                    total = total + last_in[part, k, j].astype(F32)
                own_ref[2 * part + j] = total
        for copies in (early, late, mid, last):
            for copy in copies.values():
                copy.wait_send()
        for copy in pairs:
            copy.wait_send()

    vmem = pl.BlockSpec(memory_space=pltpu.VMEM)
    tail = (3, 8, 128)
    own = pl.pallas_call(
        kernel,
        out_shape=jax.ShapeDtypeStruct((6,) + tail, F32),
        in_specs=[vmem, vmem],
        out_specs=vmem,
        scratch_shapes=[
            pltpu.VMEM((2, 6, 4, 4, 4) + tail, BF),
            pltpu.VMEM((6, 4, 4, 4) + tail, BF),
            pltpu.VMEM((3, 2, 4, 4) + tail, BF),
            pltpu.VMEM((3, 2, 2, 4, 4) + tail, BF),
            pltpu.VMEM((3, 3, 2, 4) + tail, BF),
            pltpu.VMEM((3, 3, 2) + tail, BF),
            pltpu.SemaphoreType.DMA((2, 3)),
            pltpu.SemaphoreType.DMA((2, 3, 4)),
            pltpu.SemaphoreType.DMA((2, 3, 3)),
            pltpu.SemaphoreType.DMA((2, 3, 3)),
        ],
        compiler_params=pltpu.CompilerParams(collective_id=1, has_side_effects=True, vmem_limit_bytes=60 << 20),
        name="scatter_grads",
    )(first, second)
    return from_blocks(own)


RADIUS = 6
SIDES = ((-1, -1), (-1, 0), (-1, 1), (0, -1), (0, 1), (1, -1), (1, 0), (1, 1))
OWN_ROWS = {-1: (0, 6), 0: (0, 16), 1: (10, 6)}
OWN_COLS = {-1: (0, 8), 0: (0, 32), 1: (24, 8)}
HALO_ROWS = {-1: (0, 6), 0: (6, 16), 1: (22, 6)}
HALO_COLS = {-1: (0, 8), 0: (8, 32), 1: (40, 8)}


def cut(table, step):
    first, count = table[step]
    return slice(first, first + count)


def beside(row_step, col_step):
    lat = (lax.axis_index("lat") + row_step + 8) % 8
    lon = (lax.axis_index("lon") + col_step + 16) % 16
    return (lat, lon)


def neighbours():
    return [beside(a, b) for a, b in SIDES]


def window_bias(bias, start_of):
    lat = lax.axis_index("lat")
    shape = (32, 32, 128)

    def body(i, carry):
        group, part = i // 8, i % 8
        key_row = lat * 16 + start_of(group) - 6 + part * 2 + lax.broadcasted_iota(jnp.int32, (2, 32, 128), 0)
        key_col = lax.broadcasted_iota(jnp.int32, (2, 32, 128), 1)
        lane = lax.broadcasted_iota(jnp.int32, (2, 32, 128), 2) & 63
        query_row = lat * 16 + group * 4 + (lane >> 4)
        first = jnp.clip(query_row - RADIUS, 0, 128 - 2 * RADIUS - 1)
        apart = key_col - 8 - (lane & 15)
        good = (key_row >= first) & (key_row <= first + 2 * RADIUS) & (apart >= -RADIUS) & (apart <= RADIUS)
        bias[group, pl.ds(part * 64, 64)] = jnp.where(good, 0.0, -1e30).astype(F32).reshape(64, 128)
        return carry

    lax.fori_loop(0, 32, body, 0)


def dot(a, b, left, right):
    return lax.dot_general(a, b, (((left,), (right,)), ((), ())), preferred_element_type=F32)


def spread(rows):
    head = lax.broadcasted_iota(jnp.int32, (64, 256), 1) >> 6
    return jnp.concatenate([jnp.where(head == h, rows, 0) for h in range(4)], axis=0)


def gathered(full):
    head = lax.broadcasted_iota(jnp.int32, (64, 256), 1) >> 6
    out = full[0:64]
    for h in range(1, 4):
        out = jnp.where(head == h, full[64 * h : 64 * h + 64], out)
    return out


def attend(xext, grad_output, qkv_full, out_full):
    def kernel(
        x_ref, go_ref, wqkv_ref, wout_ref, att_ref, gp_ref, q, g, k, v, dk, dv, bias, out_s, out_c, out_r, in_s, in_c,
        in_r, ssem, rsem,
    ):
        lat = lax.axis_index("lat")
        low = jnp.where(lat == 0, 4, 0)
        high = jnp.where(lat == 7, 8, 12)

        def start_of(group):
            return jnp.clip(group * 4, low, high)

        meet(neighbours())
        window_bias(bias, start_of)

        def project_own(i, carry):
            rows = x_ref[pl.ds(6 + 4 * i, 4), 8:40].reshape(128, 768)
            grads = go_ref[pl.ds(4 * i, 4)].reshape(128, 768)
            for t in range(3):
                cols = slice(256 * t, 256 * t + 256)
                head = dot(rows, wqkv_ref[:, cols], 1, 0).astype(BF).astype(F32) * 0.125
                q[t, pl.ds(4 * i, 4)] = head.astype(BF).reshape(4, 32, 256)
                head = dot(grads, wout_ref[cols, :], 1, 1).astype(BF)
                g[t, pl.ds(4 * i, 4)] = head.reshape(4, 32, 256)
            return carry

        lax.fori_loop(0, 4, project_own, 0)

        def project_all(i, carry):
            rows = x_ref[pl.ds(4 * i, 4)].reshape(192, 768)
            for t in range(3):
                for ref, first in ((k, 768), (v, 1536)):
                    cols = slice(first + 256 * t, first + 256 * t + 256)
                    ref[t, pl.ds(4 * i, 4)] = dot(rows, wqkv_ref[:, cols], 1, 0).astype(BF).reshape(4, 48, 256)
            for t in range(3):
                dk[t, pl.ds(4 * i, 4)] = jnp.zeros((4, 48, 256), F32)
                dv[t, pl.ds(4 * i, 4)] = jnp.zeros((4, 48, 256), F32)
            return carry

        lax.fori_loop(0, 7, project_all, 0)

        def tile(t, group):
            start = start_of(group)
            lanes = pl.ds(pl.multiple_of(t * 256, 256), 256)
            mask = bias[group]
            mask = jnp.concatenate([mask, mask], axis=1)
            for j in range(2):
                q_cols, k_cols = slice(16 * j, 16 * j + 16), slice(16 * j, 16 * j + 32)
                q_b = spread(q[t, pl.ds(4 * group, 4), q_cols].reshape(64, 256))
                g_b = spread(g[t, pl.ds(4 * group, 4), q_cols].reshape(64, 256))
                k4 = k[t, pl.ds(start, 16), k_cols].reshape(512, 256)
                v4 = v[t, pl.ds(start, 16), k_cols].reshape(512, 256)
                scores = dot(k4, q_b, 1, 1) + mask
                top = jnp.max(scores, axis=0, keepdims=True)
                terms = jnp.exp(scores - top)
                probs = terms * (1.0 / jnp.sum(terms, axis=0, keepdims=True))
                probs_b = probs.astype(BF)
                att = gathered(dot(probs_b, v4, 0, 0)).astype(BF)
                att_ref[pl.ds(4 * group, 4), q_cols, lanes] = att.reshape(4, 16, 256)
                dprob = dot(v4, g_b, 1, 1)
                row_term = jnp.sum(probs * dprob, axis=0, keepdims=True)
                dscore = (probs * (dprob - row_term)).astype(BF)
                dq = gathered(dot(dscore, k4, 0, 0)) * 0.125
                gp_ref[pl.ds(4 * group, 4), q_cols, lanes] = dq.astype(BF).reshape(4, 16, 256)
                dk[t, pl.ds(start, 16), k_cols] += dot(dscore, q_b, 1, 0).reshape(16, 32, 256)
                dv[t, pl.ds(start, 16), k_cols] += dot(probs_b, g_b, 1, 0).reshape(16, 32, 256)

        def slot(side, out, t):
            row_step, col_step = SIDES[side]
            if row_step == 0:
                return (out_s if out else in_s).at[0 if col_step < 0 else 1, t]
            if col_step == 0:
                return (out_r if out else in_r).at[0 if row_step < 0 else 1, t]
            return (out_c if out else in_c).at[(0 if row_step < 0 else 2) + (0 if col_step < 0 else 1), t]

        def message(side, t):
            return pltpu.make_async_remote_copy(
                src_ref=slot(side, True, t),
                dst_ref=slot(7 - side, False, t),
                send_sem=ssem.at[side, t],
                recv_sem=rsem.at[side, t],
                device_id=beside(*SIDES[side]),
                device_id_type=MESH,
            )

        def emit(sides, t):
            for side in sides:
                rows, cols = cut(HALO_ROWS, SIDES[side][0]), cut(HALO_COLS, SIDES[side][1])
                for which, ref in ((0, dk), (1, dv)):
                    slot(side, True, t)[which] = ref[t, rows, cols].astype(BF)
                message(side, t).start()

        def heads(t, carry):
            lax.fori_loop(0, 2, lambda i, c: (tile(t, i), c)[1], 0)
            emit((1, 0, 2), t)
            lax.fori_loop(2, 4, lambda i, c: (tile(t, i), c)[1], 0)
            emit((6, 5, 7, 3, 4), t)
            return carry

        lax.fori_loop(0, 3, heads, 0)

        def finish(t, carry):
            for side, (row_step, col_step) in enumerate(SIDES):
                message(side, t).wait_recv()
                r0, nr = OWN_ROWS[-row_step]
                c0, nc = OWN_COLS[-col_step]
                for which, ref in ((0, dk), (1, dv)):
                    ref[t, 6 + r0 : 6 + r0 + nr, 8 + c0 : 8 + c0 + nc] += slot(7 - side, False, t)[which].astype(F32)
            for first, ref in ((768, dk), (1536, dv)):
                lanes = pl.ds(pl.multiple_of(first + 256 * t, 256), 256)
                gp_ref[:, :, lanes] = ref[t, 6:22, 8:40].astype(BF)
            return carry

        lax.fori_loop(0, 3, finish, 0)
        for t in range(3):
            for side in range(8):
                message(side, t).wait_send()

    vmem = pl.BlockSpec(memory_space=pltpu.VMEM)
    return pl.pallas_call(
        kernel,
        out_shape=(jax.ShapeDtypeStruct((16, 32, 768), BF), jax.ShapeDtypeStruct((16, 32, 2304), BF)),
        in_specs=[vmem] * 4,
        out_specs=(vmem, vmem),
        scratch_shapes=[
            pltpu.VMEM((3, 16, 32, 256), BF),
            pltpu.VMEM((3, 16, 32, 256), BF),
            pltpu.VMEM((3, 28, 48, 256), BF),
            pltpu.VMEM((3, 28, 48, 256), BF),
            pltpu.VMEM((3, 28, 48, 256), F32),
            pltpu.VMEM((3, 28, 48, 256), F32),
            pltpu.VMEM((4, 512, 128), F32),
            pltpu.VMEM((2, 3, 2, 16, 8, 256), BF),
            pltpu.VMEM((4, 3, 2, 6, 8, 256), BF),
            pltpu.VMEM((2, 3, 2, 6, 32, 256), BF),
            pltpu.VMEM((2, 3, 2, 16, 8, 256), BF),
            pltpu.VMEM((4, 3, 2, 6, 8, 256), BF),
            pltpu.VMEM((2, 3, 2, 6, 32, 256), BF),
            pltpu.SemaphoreType.DMA((8, 3)),
            pltpu.SemaphoreType.DMA((8, 3)),
        ],
        compiler_params=pltpu.CompilerParams(collective_id=2, has_side_effects=True, vmem_limit_bytes=60 << 20),
        name="attend",
    )(xext, grad_output, qkv_full, out_full)


def shards(features, grad_output, qkv_weight, out_weight):
    qkv_full, out_full, xext = gather(to_blocks(qkv_weight, out_weight), features)
    attended, grad_proj = attend(xext, grad_output, qkv_full, out_full)
    x_rows = features.reshape(-1, 768)
    grad_rows = grad_output.reshape(-1, 768)
    grad_proj = grad_proj.reshape(-1, 2304)
    grad_features = lax.dot_general(
        grad_proj, qkv_full, (((1,), (1,)), ((), ())), preferred_element_type=F32
    )
    grad_features = grad_features.astype(BF).reshape(16, 32, 768)
    first_term = lax.dot_general(x_rows, grad_proj, (((0,), (0,)), ((), ())), preferred_element_type=F32)
    second_term = lax.dot_general(
        attended.reshape(-1, 768), grad_rows, (((0,), (0,)), ((), ())), preferred_element_type=F32
    )
    my_grads = scatter(first_term, second_term)
    return (grad_features, my_grads[:, :2304], my_grads[:, 2304:])


def solution(mesh):
    placed = (P("lat", "lon", None), P("lat", "lon", None), P(("lat", "lon"), None), P(("lat", "lon"), None))
    return jax.shard_map(
        shards,
        mesh=mesh,
        in_specs=placed,
        out_specs=(P("lat", "lon", None), P(("lat", "lon"), None), P(("lat", "lon"), None)),
        check_vma=False,
    )
```

time: 205 us -> 163 us (0.80)
  Pallas kernels: 188 us -> 145 us
    pallas_call x1, Pallas kernels: 63.1 us -> 46.4 us  [gather(): pl.pallas_call(kernel, out_shape=(jax.ShapeDtypeStruct((768, 2304), BF),...]
    pallas_call x1, Pallas kernels: 82.7 us -> 68.5 us  [attend(): pl.pallas_call(kernel, out_shape=(jax.ShapeDtypeStruct((16, 32, 768), BF)...]
    pallas_call x1, Pallas kernels: 42.3 us -> 30.4 us  [scatter(): pl.pallas_call(kernel, out_shape=jax.ShapeDtypeStruct((6,) + tail, F32),...]
where the time goes in v3:
time: 163 us; the launch traced here: 162 us
  Pallas kernels  145 us (89%)
  matrix products  12 us (7%)
  local copies, waits for them, and re-layouts  2.8 us (2%)
    pallas_call x1, Pallas kernels, attend(): pl.pallas_call(kernel, out_shape=(jax.ShapeDtypeStruct((16, 32, 768), BF)...  68.5 us
    pallas_call x1, Pallas kernels, gather(): pl.pallas_call(kernel, out_shape=(jax.ShapeDtypeStruct((768, 2304), BF),...  46.4 us
    pallas_call x1, Pallas kernels, scatter(): pl.pallas_call(kernel, out_shape=jax.ShapeDtypeStruct((6,) + tail, F32),...  30.4 us
    dot_general x1, matrix products, shards(): lax.dot_general(x_rows, grad_proj, (((0,), (0,)), ((), ())), preferred_el...  4.97 us
    dot_general x1, matrix products, shards(): lax.dot_general(grad_proj, qkv_full, (((1,), (1,)), ((), ())), preferred_...  4.72 us

profile of v3, /device:TPU:1, one launch (start us, length us, event | category | flops | bytes accessed | tf_op | source)
XLA Modules:
  0.0 161.6 jit_solution(13485605928534397441)
XLA Ops:
  0.6 0.8 pad_maximum_fusion
  1.4 0.6 reshape.28.own_ref
  2.1 46.4 %gather_weights.1 = (bf16[768,2304]{1,0:T(8,128)(2,1)}, bf16[768,768]{1,0:T(8,128)(2,1)}, bf16[28,48,768]{2,1,0:T(8,128)(2,1)}) custom-call(bf16[6,3,8,128]{3,2,1,0:T(8,128)(2,1)} %reshape.28.own_ref, bf16[16,32,768]{2,1,0:T(8,128)(2,1)} %x_ref.1), custom_call_target="tpu_custom_call" | custom-call | tf_op jit(solution)/shard_map/gather_weights/pallas_call | solution.py:178
  48.5 0.0 copy-start
  48.5 68.5 %attend.1 = (bf16[16,32,768]{2,1,0:T(8,128)(2,1)}, bf16[16,32,2304]{2,1,0:T(8,128)(2,1)}) custom-call(bf16[28,48,768]{2,1,0:T(8,128)(2,1)} %get-tuple-element.8.x_ref, bf16[16,32,768]{2,1,0:T(8,128)(2,1)} %go_ref.1, bf16[768,2304]{1,0:T(8,128)(2,1)} %get-tuple-element.9.wqkv_ref, bf16[768,768]{1,0:T(8,128)(2,1)} %get-tuple-element.10.wout_ref), custom_call_target="tpu_custom_call" | custom-call | tf_op jit(solution)/shard_map/attend/pallas_call | solution.py:539
  117.1 0.0 copy-done
  117.1 0.0 copy-start.1
  117.1 0.0 copy-start.2
  117.1 4.7 %convolution_convert_fusion = bf16[512,768]{1,0:T(8,128)(2,1)} fusion(bf16[512,2304]{1,0:T(8,128)(2,1)} %bitcast.22, bf16[768,2304]{1,0:T(8,128)(2,1)S(1)} %copy-done), kind=kOutput, calls=%fused_computation.2 | convolution fusion | flops 1812332544 | bytes 6684672 | tf_op jit(solution)/shard_map/dot_general | solution.py:572
  121.8 0.0 copy-done.1
  121.8 0.0 copy-done.2
  121.8 0.0 copy-start.3
  121.8 0.0 copy-start.4
  121.8 5.0 %convolution_bitcast_fusion.qkv_ref = f32[768,2304]{1,0:T(8,128)} fusion(bf16[16,32,2304]{2,1,0:T(8,128)(2,1)S(1)} %copy-done.2, bf16[16,32,768]{2,1,0:T(8,128)(2,1)S(1)} %copy-done.1), kind=kOutput, calls=%fused_computation | convolution fusion | flops 1811939328 | bytes 10223616 | tf_op jit(solution)/shard_map/dot_general | solution.py:576
  126.8 0.0 copy-done.3
  126.8 0.0 copy-done.4
  126.8 2.3 %convolution_bitcast_fusion.1.out_ref = f32[768,768]{1,0:T(8,128)} fusion(bf16[16,32,768]{2,1,0:T(8,128)(2,1)S(1)} %copy-done.4, bf16[16,32,768]{2,1,0:T(8,128)(2,1)S(1)} %copy-done.3), kind=kOutput, calls=%fused_computation.1 | convolution fusion | flops 603979776 | bytes 3932160 | tf_op jit(solution)/shard_map/dot_general | solution.py:577
  129.1 30.4 %scatter_grads.1 = f32[6,3,8,128]{3,2,1,0:T(8,128)} custom-call(f32[768,2304]{1,0:T(8,128)} %convolution_bitcast_fusion.qkv_ref, f32[768,768]{1,0:T(8,128)} %convolution_bitcast_fusion.1.out_ref), custom_call_target="tpu_custom_call" | custom-call | tf_op jit(solution)/shard_map/scatter_grads/pallas_call | solution.py:338
  159.5 0.9 reshape.31
  160.4 0.6 slice.8
  161.0 0.6 slice.9
Async XLA Ops:
  48.5 68.6 %copy-start = (bf16[768,2304]{1,0:T(8,128)(2,1)S(1)}, bf16[768,2304]{1,0:T(8,128)(2,1)}, u32[]{:S(2)}) copy-start(bf16[768,2304]{1,0:T(8,128)(2,1)} %get-tuple-element.9.wqkv_ref) | copy-start | bytes 10616836
  117.1 4.7 %copy-start.1 = (bf16[16,32,768]{2,1,0:T(8,128)(2,1)S(1)}, bf16[16,32,768]{2,1,0:T(8,128)(2,1)}, u32[]{:S(2)}) copy-start(bf16[16,32,768]{2,1,0:T(8,128)(2,1)} %x_ref.1) | copy-start | bytes 2359300
  117.1 4.7 %copy-start.2 = (bf16[16,32,2304]{2,1,0:T(8,128)(2,1)S(1)}, bf16[16,32,2304]{2,1,0:T(8,128)(2,1)}, u32[]{:S(2)}) copy-start(bf16[16,32,2304]{2,1,0:T(8,128)(2,1)} %get-tuple-element.11) | copy-start | bytes 7077892
  121.8 5.0 %copy-start.3 = (bf16[16,32,768]{2,1,0:T(8,128)(2,1)S(1)}, bf16[16,32,768]{2,1,0:T(8,128)(2,1)}, u32[]{:S(2)}) copy-start(bf16[16,32,768]{2,1,0:T(8,128)(2,1)} %go_ref.1) | copy-start | bytes 2359300
  121.8 5.0 %copy-start.4 = (bf16[16,32,768]{2,1,0:T(8,128)(2,1)S(1)}, bf16[16,32,768]{2,1,0:T(8,128)(2,1)}, u32[]{:S(2)}) copy-start(bf16[16,32,768]{2,1,0:T(8,128)(2,1)} %get-tuple-element.12) | copy-start | bytes 2359300

commit v4 on v3

v4 whole, which is shorter than its diff:
```python
import jax
import jax.numpy as jnp
from jax import lax
from jax.experimental import pallas as pl
from jax.experimental.pallas import tpu as pltpu
from jax.sharding import PartitionSpec as P

MESH = pl.DeviceIdType.MESH
BF = jnp.bfloat16
F32 = jnp.float32


def place():
    lat = lax.axis_index("lat")
    lon = lax.axis_index("lon")
    z, x_lo = lat // 2, lat % 2
    y, x_hi, core = lon // 4, (lon // 2) % 2, lon % 2
    return {"z": z, "y": y, "x": x_hi * 2 + x_lo}, core


def device(at, core):
    return (at["z"] * 2 + at["x"] % 2, at["y"] * 4 + (at["x"] // 2) * 2 + core)


def moved(at, axis, steps):
    out = dict(at)
    out[axis] = (at[axis] + steps + 4) % 4
    return out


def meet(peers):
    barrier = pltpu.get_barrier_semaphore()
    for peer in peers:
        pl.semaphore_signal(barrier, inc=1, device_id=peer, device_id_type=MESH)
    pl.semaphore_wait(barrier, len(peers))


def torus_peers(at, core):
    peers = [device(at, 1 - core)]
    for axis in ("z", "y", "x"):
        for steps in (1, 2, 3):
            peers.append(device(moved(at, axis, steps), core))
    return peers


def region(at, full, axis=None, coord=None):
    index = []
    for name in ("z", "y", "x"):
        if name == axis:
            index.append(coord)
        elif name in full:
            index.append(slice(None))
        else:
            index.append(at[name])
    return tuple(index)


def send(src, dst, ssem, rsem, peer):
    copy = pltpu.make_async_remote_copy(
        src_ref=src, dst_ref=dst, send_sem=ssem, recv_sem=rsem, device_id=peer, device_id_type=MESH
    )
    copy.start()
    return copy


def unpack(blocks, write):
    def body(step, carry):
        z, rest = step // 4, step % 4
        x_lo, y_pair = rest // 2, rest % 2
        for unit in range(6):
            pieces = []
            for y in range(2):
                for x_hi in range(2):
                    for core in range(2):
                        piece = blocks[core, unit, z, 2 * y_pair + y, 2 * x_hi + x_lo]
                        pieces.append(piece.astype(F32).reshape(24, 128))
            for chunk in range(4):
                rows = jnp.concatenate([p[6 * chunk : 6 * chunk + 6] for p in pieces], axis=0)
                write(step, 4 * unit + chunk, rows.astype(BF))
        return carry

    lax.fori_loop(0, 16, body, 0)


GATHER_PARTS = ((0, 4, "z", "y"), (4, 2, "y", "z"))


def gather(own, features):
    def kernel(
        own_ref, x_ref, qkv_ref, out_ref, ext_ref, blocks, sem1, sem2, sem3, psem, local_sem, hssem, hrsem
    ):
        at, core = place()
        z, y, x = at["z"], at["y"], at["x"]
        local = pltpu.make_async_copy(own_ref, blocks.at[core, :, z, y, x], local_sem.at[0])
        local.start()
        inner = pltpu.make_async_copy(x_ref, ext_ref.at[6:22, 8:40], local_sem.at[1])
        inner.start()
        meet(torus_peers(at, core) + neighbours())
        partner = device(at, 1 - core)
        sent = []
        first = []
        for k in range(3):
            first.append(
                send(
                    own_ref, blocks.at[core, :, z, y, x], sem1.at[0, k], sem1.at[1, k],
                    device(moved(at, "x", k + 1), core),
                )
            )
        halos = []
        for side, (row_step, col_step) in enumerate(SIDES):
            src = x_ref.at[cut(OWN_ROWS, row_step), cut(OWN_COLS, col_step)]
            dst = ext_ref.at[cut(HALO_ROWS, -row_step), cut(HALO_COLS, -col_step)]
            halos.append(send(src, dst, hssem.at[side], hrsem.at[side], beside(row_step, col_step)))
        local.wait()
        for copy in first:
            copy.wait_recv()
        second = {}
        for part, (unit, count, axis, _) in enumerate(GATHER_PARTS):
            where = (core, slice(unit, unit + count)) + region(at, "x")
            for k in range(3):
                second[part, k] = send(
                    blocks.at[where], blocks.at[where], sem2.at[0, part, k], sem2.at[1, part, k],
                    device(moved(at, axis, k + 1), core),
                )
        third, passed = {}, []

        def hand(part, k, where):
            passed.append(
                send(blocks.at[where], blocks.at[where], psem.at[0, part, k], psem.at[1, part, k], partner)
            )

        for part, (unit, count, axis, last) in enumerate(GATHER_PARTS):
            for k in range(3):
                second[part, k].wait_recv()
            where = (core, slice(unit, unit + count)) + region(at, ("x", axis), last, at[last])
            for k, steps in ((0, 1), (1, -1)):
                third[part, k] = send(
                    blocks.at[where], blocks.at[where], sem3.at[0, part, k], sem3.at[1, part, k],
                    device(moved(at, last, steps), core),
                )
            hand(part, 0, where)
        for part, (unit, count, axis, last) in enumerate(GATHER_PARTS):
            for k, steps in ((0, 1), (1, -1)):
                third[part, k].wait_recv()
                back = region(at, ("x", axis), last, (at[last] - steps + 4) % 4)
                half = count // 2
                where = (core, slice(unit + k * half, unit + k * half + half)) + back
                third[part, 2 + k] = send(
                    blocks.at[where], blocks.at[where], sem3.at[0, part, 2 + k], sem3.at[1, part, 2 + k],
                    device(moved(at, last, steps), core),
                )
                hand(part, 1 + k, (core, slice(unit, unit + count)) + back)
        for part, (unit, count, axis, last) in enumerate(GATHER_PARTS):
            half = count // 2
            far = region(at, ("x", axis), last, (at[last] + 2) % 4)
            for k in range(2):
                third[part, 2 + k].wait_recv()
                hand(part, 3 + k, (core, slice(unit + k * half, unit + k * half + half)) + far)
        for copy in passed:
            copy.wait_recv()

        def write(step, chunk, rows):
            first_row = pl.multiple_of(step * 48, 16)
            if chunk < 18:
                qkv_ref[pl.ds(first_row, 48), 128 * chunk : 128 * chunk + 128] = rows
            else:
                chunk -= 18
                out_ref[pl.ds(first_row, 48), 128 * chunk : 128 * chunk + 128] = rows

        unpack(blocks, write)
        for copy in halos:
            copy.wait_recv()
        for copy in halos + first + list(second.values()) + list(third.values()) + passed:
            copy.wait_send()
        inner.wait()

    vmem = pl.BlockSpec(memory_space=pltpu.VMEM)
    return pl.pallas_call(
        kernel,
        out_shape=(
            jax.ShapeDtypeStruct((768, 2304), BF),
            jax.ShapeDtypeStruct((768, 768), BF),
            jax.ShapeDtypeStruct((28, 48, 768), BF),
        ),
        in_specs=[vmem, vmem],
        out_specs=(vmem, vmem, vmem),
        scratch_shapes=[
            pltpu.VMEM((2, 6, 4, 4, 4, 3, 8, 128), BF),
            pltpu.SemaphoreType.DMA((2, 3)),
            pltpu.SemaphoreType.DMA((2, 2, 3)),
            pltpu.SemaphoreType.DMA((2, 2, 4)),
            pltpu.SemaphoreType.DMA((2, 2, 5)),
            pltpu.SemaphoreType.DMA((2,)),
            pltpu.SemaphoreType.DMA((8,)),
            pltpu.SemaphoreType.DMA((8,)),
        ],
        compiler_params=pltpu.CompilerParams(collective_id=0, has_side_effects=True),
        name="gather_weights",
    )(own, features)


def to_blocks(qkv, out):
    rows = jnp.concatenate([qkv, out], axis=1)
    rows = rows.reshape(6, 6, 4, 128).transpose(1, 2, 0, 3)
    return rows.reshape(6, 3, 8, 128)


RADIUS = 6
SIDES = ((-1, -1), (-1, 0), (-1, 1), (0, -1), (0, 1), (1, -1), (1, 0), (1, 1))
OWN_ROWS = {-1: (0, 6), 0: (0, 16), 1: (10, 6)}
OWN_COLS = {-1: (0, 8), 0: (0, 32), 1: (24, 8)}
HALO_ROWS = {-1: (0, 6), 0: (6, 16), 1: (22, 6)}
HALO_COLS = {-1: (0, 8), 0: (8, 32), 1: (40, 8)}


def cut(table, step):
    first, count = table[step]
    return slice(first, first + count)


def beside(row_step, col_step):
    lat = (lax.axis_index("lat") + row_step + 8) % 8
    lon = (lax.axis_index("lon") + col_step + 16) % 16
    return (lat, lon)


def neighbours():
    return [beside(a, b) for a, b in SIDES]


def window_bias(bias, start_of):
    lat = lax.axis_index("lat")
    shape = (32, 32, 128)

    def body(i, carry):
        group, part = i // 8, i % 8
        key_row = lat * 16 + start_of(group) - 6 + part * 2 + lax.broadcasted_iota(jnp.int32, (2, 32, 128), 0)
        key_col = lax.broadcasted_iota(jnp.int32, (2, 32, 128), 1)
        lane = lax.broadcasted_iota(jnp.int32, (2, 32, 128), 2) & 63
        query_row = lat * 16 + group * 4 + (lane >> 4)
        first = jnp.clip(query_row - RADIUS, 0, 128 - 2 * RADIUS - 1)
        apart = key_col - 8 - (lane & 15)
        good = (key_row >= first) & (key_row <= first + 2 * RADIUS) & (apart >= -RADIUS) & (apart <= RADIUS)
        bias[group, pl.ds(part * 64, 64)] = jnp.where(good, 0.0, -1e30).astype(F32).reshape(64, 128)
        return carry

    lax.fori_loop(0, 32, body, 0)


def dot(a, b, left, right):
    return lax.dot_general(a, b, (((left,), (right,)), ((), ())), preferred_element_type=F32)


def spread(rows):
    head = lax.broadcasted_iota(jnp.int32, (64, 256), 1) >> 6
    return jnp.concatenate([jnp.where(head == h, rows, 0) for h in range(4)], axis=0)


def gathered(full):
    head = lax.broadcasted_iota(jnp.int32, (64, 256), 1) >> 6
    out = full[0:64]
    for h in range(1, 4):
        out = jnp.where(head == h, full[64 * h : 64 * h + 64], out)
    return out


def chunk_column(i):
    return 768 * (i % 3) + 256 * (i // 3) if i < 9 else 256 * (i - 9)


SCATTER_ORDERS = (("x", "y", "z"), ("y", "z", "x"), ("z", "y", "x"))


def attend(xext, grad_output, qkv_full, out_full):
    def kernel(
        x_ref, go_ref, wqkv_ref, wout_ref, gx_ref, gqkv_ref, gout_ref,
        q, g, k, v, dk, dv, bias, att, dq, dkv, xt, xo, dw, dx, out_s, out_c, out_r, in_s, in_c, in_r,
        blocks, pair_in, half_in, whole_in, mid_in, last_in, hsem, psem, ssem, msem, lsem,
    ):
        at, core = place()
        partner = device(at, 1 - core)
        lat = lax.axis_index("lat")
        low = jnp.where(lat == 0, 4, 0)
        high = jnp.where(lat == 7, 8, 12)

        def start_of(group):
            return jnp.clip(group * 4, low, high)

        def each(count, body):
            lax.fori_loop(0, count, lambda i, c: (body(i), c)[1], 0)

        meet(torus_peers(at, core) + neighbours())
        window_bias(bias, start_of)

        def project_own(t):
            lanes = pl.ds(pl.multiple_of(256 * t, 256), 256)
            rows = x_ref[6:22, 8:40].reshape(512, 768)
            head = dot(rows, wqkv_ref[:, lanes], 1, 0).astype(BF).astype(F32) * 0.125
            q[t] = head.astype(BF).reshape(16, 32, 256)
            grads = go_ref[...].reshape(512, 768)
            g[t] = dot(grads, wout_ref[lanes, :], 1, 1).astype(BF).reshape(16, 32, 256)

        each(3, project_own)

        def project_all(i):
            t, half = i // 2, pl.ds(14 * (i % 2), 14)
            rows = x_ref[half].reshape(672, 768)
            for ref, first in ((k, 768), (v, 1536)):
                lanes = pl.ds(pl.multiple_of(first + 256 * t, 256), 256)
                ref[t, half] = dot(rows, wqkv_ref[:, lanes], 1, 0).astype(BF).reshape(14, 48, 256)

        each(6, project_all)
        for i in range(6):
            lanes = slice(128 * i, 128 * i + 128)
            xt[lanes] = x_ref[:, :, lanes].reshape(1344, 128).T
            xo[lanes] = x_ref[6:22, 8:40, lanes].reshape(512, 128).T

        def tile(t, group):
            start = start_of(group)
            lanes = slice(256 * t, 256 * t + 256)
            mask = bias[group]
            mask = jnp.concatenate([mask, mask], axis=1)
            for j in range(2):
                q_cols, k_cols = slice(16 * j, 16 * j + 16), slice(16 * j, 16 * j + 32)
                q_b = spread(q[t, pl.ds(4 * group, 4), q_cols].reshape(64, 256))
                g_b = spread(g[t, pl.ds(4 * group, 4), q_cols].reshape(64, 256))
                k4 = k[t, pl.ds(start, 16), k_cols].reshape(512, 256)
                v4 = v[t, pl.ds(start, 16), k_cols].reshape(512, 256)
                scores = dot(k4, q_b, 1, 1) + mask
                top = jnp.max(scores, axis=0, keepdims=True)
                terms = jnp.exp(scores - top)
                probs = terms * (1.0 / jnp.sum(terms, axis=0, keepdims=True))
                probs_b = probs.astype(BF)
                out = gathered(dot(probs_b, v4, 0, 0)).astype(BF)
                att[pl.ds(4 * group, 4), q_cols, lanes] = out.reshape(4, 16, 256)
                dprob = dot(v4, g_b, 1, 1)
                row_term = jnp.sum(probs * dprob, axis=0, keepdims=True)
                dscore = (probs * (dprob - row_term)).astype(BF)
                out = gathered(dot(dscore, k4, 0, 0)) * 0.125
                dq[pl.ds(4 * group, 4), q_cols, lanes] = out.astype(BF).reshape(4, 16, 256)
                dk[pl.ds(start, 16), k_cols] += dot(dscore, q_b, 1, 0).reshape(16, 32, 256)
                dv[pl.ds(start, 16), k_cols] += dot(probs_b, g_b, 1, 0).reshape(16, 32, 256)

        pairs, early, late, mid, last = {}, {}, {}, {}, {}

        def begin(part):
            for i in range(4 * part, 4 * part + 4):
                to = slice(256 * (i % 4), 256 * (i % 4) + 256)
                col = chunk_column(i)

                if i >= 9:
                    left = att[...].reshape(512, 768)
                    dw[:, to] = dot(left, go_ref[:, :, col : col + 256].reshape(512, 256), 0, 0)
                elif i % 3 == 0:
                    dw[:, to] = dot(xo[...], dq[:, :, col : col + 256].reshape(512, 256), 1, 0)
                else:
                    dw[:, to] = dot(xt[...], dkv[:, :, col - 768 : col - 512].reshape(1344, 256), 1, 0)

            def pack(step):
                z, rest = step // 4, step % 4
                x_lo, y_pair = rest // 2, rest % 2
                first_row = pl.multiple_of(step * 48, 16)
                for unit in range(2):
                    chunks = []
                    for n in range(4):
                        first = 512 * unit + 128 * n
                        chunks.append(dw[pl.ds(first_row, 48), first : first + 128])
                    for e in range(8):
                        y, x_hi, to = e // 4, (e // 2) % 2, e % 2
                        rows = jnp.concatenate([c[6 * e : 6 * e + 6] for c in chunks], axis=0)
                        rows = rows.reshape(3, 8, 128).astype(BF)
                        blocks[to, 2 * part + unit, z, 2 * y_pair + y, 2 * x_hi + x_lo] = rows

            each(16, pack)
            units = slice(2 * part, 2 * part + 2)
            pairs[part] = send(
                blocks.at[1 - core, units], pair_in.at[units], psem.at[0, part], psem.at[1, part], partner
            )

        def step_pair(part):
            a0, a1, a2 = SCATTER_ORDERS[part]
            pairs[part].wait_recv()

            def add(i):
                unit, z = 2 * part + i // 4, i % 4
                total = blocks[core, unit, z].astype(F32) + pair_in[unit, z].astype(F32)
                blocks[core, unit, z] = total.astype(BF)

            each(8, add)
            far = region(at, (a1, a2), a0, (at[a0] + 2) % 4)
            for n, steps in ((0, 1), (1, -1)):
                early[part, n] = send(
                    blocks.at[(core, 2 * part + n) + far], half_in.at[part, n], ssem.at[0, part, n],
                    ssem.at[1, part, n], device(moved(at, a0, steps), core),
                )

        def step_early(part):
            a0, a1, a2 = SCATTER_ORDERS[part]
            for n, steps in ((0, 1), (1, -1)):
                early[part, n].wait_recv()
                near = region(at, (a1, a2), a0, (at[a0] + steps + 4) % 4)

                here = (core, 2 * part + n) + near
                blocks[here] = (blocks[here].astype(F32) + half_in[part, n].astype(F32)).astype(BF)
                late[part, n] = send(
                    blocks.at[(core, slice(2 * part, 2 * part + 2)) + near], whole_in.at[part, n],
                    ssem.at[0, part, 2 + n], ssem.at[1, part, 2 + n], device(moved(at, a0, steps), core),
                )

        def step_late(part):
            a0, a1, a2 = SCATTER_ORDERS[part]
            late[part, 0].wait_recv()
            late[part, 1].wait_recv()
            mine = region(at, (a1, a2), a0, at[a0])

            for j in range(2):
                here = (core, 2 * part + j) + mine
                total = blocks[here].astype(F32) + whole_in[part, 0, j].astype(F32)
                blocks[here] = (total + whole_in[part, 1, j].astype(F32)).astype(BF)
            for n in range(3):
                where = region(at, (a2,), a1, (at[a1] + n + 1) % 4)
                mid[part, n] = send(
                    blocks.at[(core, slice(2 * part, 2 * part + 2)) + where], mid_in.at[part, n],
                    msem.at[0, part, n], msem.at[1, part, n], device(moved(at, a1, n + 1), core),
                )

        def step_mid(part):
            a0, a1, a2 = SCATTER_ORDERS[part]
            for n in range(3):
                mid[part, n].wait_recv()
            mine = region(at, (a2,), a1, at[a1])
            for j in range(2):
                here = (core, 2 * part + j) + mine
                total = blocks[here].astype(F32)
                for n in range(3):
                    total = total + mid_in[part, n, j].astype(F32)
                blocks[here] = total.astype(BF)
            for n in range(3):
                where = region(at, (), a2, (at[a2] + n + 1) % 4)
                last[part, n] = send(
                    blocks.at[(core, slice(2 * part, 2 * part + 2)) + where], last_in.at[part, n],
                    lsem.at[0, part, n], lsem.at[1, part, n], device(moved(at, a2, n + 1), core),
                )

        def step_last(part):
            for n in range(3):
                last[part, n].wait_recv()
            for j in range(2):
                total = blocks[(core, 2 * part + j) + region(at, ())].astype(F32)
                for n in range(3):
                    total = total + last_in[part, n, j].astype(F32)
                total = total.reshape(24, 128)
                for n in range(4):
                    i = 4 * part + 2 * j + n // 2
                    col = chunk_column(i) + 128 * (n % 2)
                    ref = gout_ref if i >= 9 else gqkv_ref
                    ref[:, col : col + 128] = total[6 * n : 6 * n + 6]

        for t in range(3):

            def clear(i):
                dk[i] = jnp.zeros((48, 256), F32)
                dv[i] = jnp.zeros((48, 256), F32)

            each(28, clear)
            each(4, lambda group, t=t: tile(t, group))

            def store(i, t=t):
                dkv[i, :, 256 * t : 256 * t + 256] = dk[i].astype(BF)
                dkv[i, :, 768 + 256 * t : 1024 + 256 * t] = dv[i].astype(BF)

            each(28, store)
            if t == 1:
                begin(0)

        def back_edge(n):
            lanes = pl.ds(pl.multiple_of(256 * n, 256), 256)
            rows = jnp.concatenate([dkv[0:6].reshape(288, 1536), dkv[22:28].reshape(288, 1536)], axis=0)
            out = dot(rows, wqkv_ref[lanes, 768:2304], 1, 1)
            dx[0:6, :, lanes] = out[0:288].reshape(6, 48, 256)
            dx[22:28, :, lanes] = out[288:576].reshape(6, 48, 256)

        def back_inner(n):
            lanes = pl.ds(pl.multiple_of(256 * n, 256), 256)
            rows = dkv[6:22].reshape(768, 1536)
            dx[6:22, :, lanes] = dot(rows, wqkv_ref[lanes, 768:2304], 1, 1).reshape(16, 48, 256)

        def back_own(n):
            lanes = pl.ds(pl.multiple_of(256 * n, 256), 256)
            rows = dq[...].reshape(512, 768)
            dx[6:22, 8:40, lanes] += dot(rows, wqkv_ref[lanes, 0:768], 1, 1).reshape(16, 32, 256)

        def slot(side, out):
            row_step, col_step = SIDES[side]
            if row_step == 0:
                return (out_s if out else in_s).at[0 if col_step < 0 else 1]
            if col_step == 0:
                return (out_r if out else in_r).at[0 if row_step < 0 else 1]
            return (out_c if out else in_c).at[(0 if row_step < 0 else 2) + (0 if col_step < 0 else 1)]

        halos = {}

        def emit(side):
            rows, cols = cut(HALO_ROWS, SIDES[side][0]), cut(HALO_COLS, SIDES[side][1])
            slot(side, True)[...] = dx[rows, cols].astype(BF)
            halos[side] = send(
                slot(side, True), slot(7 - side, False), hsem.at[0, side], hsem.at[1, side], beside(*SIDES[side])
            )

        step_pair(0)
        each(3, back_edge)
        for side in (1, 6, 0, 2, 5, 7):
            emit(side)
        begin(1)
        step_early(0)
        begin(2)
        step_pair(1)
        each(3, back_inner)
        for side in (3, 4):
            emit(side)
        step_pair(2)
        step_late(0)
        step_early(1)
        step_early(2)
        step_mid(0)

        each(3, back_own)
        step_late(1)
        step_late(2)
        step_last(0)
        step_mid(1)
        step_mid(2)
        for side, (row_step, col_step) in enumerate(SIDES):
            halos[side].wait_recv()
            r0, nr = OWN_ROWS[-row_step]
            c0, nc = OWN_COLS[-col_step]
            dx[6 + r0 : 6 + r0 + nr, 8 + c0 : 8 + c0 + nc] += slot(7 - side, False)[...].astype(F32)

        def finish(i):
            gx_ref[pl.ds(4 * i, 4)] = dx[pl.ds(6 + 4 * i, 4), 8:40].astype(BF)

        each(4, finish)
        step_last(1)
        step_last(2)
        for copies in (pairs, early, late, mid, last, halos):
            for copy in copies.values():
                copy.wait_send()

    vmem = pl.BlockSpec(memory_space=pltpu.VMEM)
    tail = (3, 8, 128)
    return pl.pallas_call(
        kernel,
        out_shape=(
            jax.ShapeDtypeStruct((16, 32, 768), BF),
            jax.ShapeDtypeStruct((6, 2304), F32),
            jax.ShapeDtypeStruct((6, 768), F32),
        ),
        in_specs=[vmem] * 4,
        out_specs=(vmem, vmem, vmem),
        scratch_shapes=[
            pltpu.VMEM((3, 16, 32, 256), BF),
            pltpu.VMEM((3, 16, 32, 256), BF),
            pltpu.VMEM((3, 28, 48, 256), BF),
            pltpu.VMEM((3, 28, 48, 256), BF),
            pltpu.VMEM((28, 48, 256), F32),
            pltpu.VMEM((28, 48, 256), F32),
            pltpu.VMEM((4, 512, 128), F32),
            pltpu.VMEM((16, 32, 768), BF),
            pltpu.VMEM((16, 32, 768), BF),
            pltpu.VMEM((28, 48, 1536), BF),
            pltpu.VMEM((768, 1344), BF),
            pltpu.VMEM((768, 512), BF),
            pltpu.VMEM((768, 1024), F32),
            pltpu.VMEM((28, 48, 768), F32),
            pltpu.VMEM((2, 16, 8, 768), BF),
            pltpu.VMEM((4, 6, 8, 768), BF),
            pltpu.VMEM((2, 6, 32, 768), BF),
            pltpu.VMEM((2, 16, 8, 768), BF),
            pltpu.VMEM((4, 6, 8, 768), BF),
            pltpu.VMEM((2, 6, 32, 768), BF),
            pltpu.VMEM((2, 6, 4, 4, 4) + tail, BF),
            pltpu.VMEM((6, 4, 4, 4) + tail, BF),
            pltpu.VMEM((3, 2, 4, 4) + tail, BF),
            pltpu.VMEM((3, 2, 2, 4, 4) + tail, BF),
            pltpu.VMEM((3, 3, 2, 4) + tail, BF),
            pltpu.VMEM((3, 3, 2) + tail, BF),
            pltpu.SemaphoreType.DMA((2, 8)),
            pltpu.SemaphoreType.DMA((2, 3)),
            pltpu.SemaphoreType.DMA((2, 3, 4)),
            pltpu.SemaphoreType.DMA((2, 3, 3)),
            pltpu.SemaphoreType.DMA((2, 3, 3)),
        ],
        compiler_params=pltpu.CompilerParams(collective_id=1, has_side_effects=True, vmem_limit_bytes=62 << 20),
        name="attend",
    )(xext, grad_output, qkv_full, out_full)


def shards(features, grad_output, qkv_weight, out_weight):
    qkv_full, out_full, xext = gather(to_blocks(qkv_weight, out_weight), features)
    return tuple(attend(xext, grad_output, qkv_full, out_full))


def solution(mesh):
    placed = (P("lat", "lon", None), P("lat", "lon", None), P(("lat", "lon"), None), P(("lat", "lon"), None))
    return jax.shard_map(
        shards,
        mesh=mesh,
        in_specs=placed,
        out_specs=(P("lat", "lon", None), P(("lat", "lon"), None), P(("lat", "lon"), None)),
        check_vma=False,
    )
```

time: 163 us -> 142 us (0.87)
  matrix products: 12 us -> 0 us
  Pallas kernels: 145 us -> 135 us
  local copies, waits for them, and re-layouts: 2.8 us -> 5.57 us
    pallas_call x1 -> x0, Pallas kernels: 30.4 us -> none  [scatter(): pl.pallas_call(kernel, out_shape=jax.ShapeDtypeStruct((6,) + tail, F32),...]
    pallas_call x1, Pallas kernels: 68.5 us -> 88.4 us  [attend(): pl.pallas_call(kernel, out_shape=(jax.ShapeDtypeStruct((16, 32, 768), BF)...]
    dot_general x3 -> x0, matrix products: 12 us -> none  [the longest x1 4.97 us: shards(): lax.dot_general(x_rows, grad_proj, (((0,), (0,)), ((), ())), preferred_el...]
    unnamed x10 -> x3, local copies, waits for them, and re-layouts: 0.02 us -> 4.93 us
where the time goes in v4:
time: 142 us
  Pallas kernels  135 us (95%)
  local copies, waits for them, and re-layouts  5.57 us (4%)
    pallas_call x1, Pallas kernels, attend(): pl.pallas_call(kernel, out_shape=(jax.ShapeDtypeStruct((16, 32, 768), BF)...  88.4 us
    pallas_call x1, Pallas kernels, gather(): pl.pallas_call(kernel, out_shape=(jax.ShapeDtypeStruct((768, 2304), BF),...  46.5 us
    unnamed x3, local copies, waits for them, and re-layouts  4.93 us

profile of v4, /device:TPU:1, one launch (start us, length us, event | category | flops | bytes accessed | tf_op | source)
XLA Modules:
  0.0 141.9 jit_solution(3312728560784696068)
XLA Ops:
  0.6 0.8 pad_maximum_fusion
  1.4 0.6 reshape.13.own_ref
  2.1 46.5 %gather_weights.1 = (bf16[768,2304]{1,0:T(8,128)(2,1)}, bf16[768,768]{1,0:T(8,128)(2,1)}, bf16[28,48,768]{2,1,0:T(8,128)(2,1)}) custom-call(bf16[6,3,8,128]{3,2,1,0:T(8,128)(2,1)} %reshape.13.own_ref, bf16[16,32,768]{2,1,0:T(8,128)(2,1)} %x_ref.1), custom_call_target="tpu_custom_call" | custom-call | tf_op jit(solution)/shard_map/gather_weights/pallas_call | solution.py:178
  48.5 88.4 %attend.1 = (bf16[16,32,768]{2,1,0:T(8,128)(2,1)}, f32[6,2304]{1,0:T(8,128)}, f32[6,768]{1,0:T(8,128)}) custom-call(bf16[28,48,768]{2,1,0:T(8,128)(2,1)} %get-tuple-element.6.x_ref, bf16[16,32,768]{2,1,0:T(8,128)(2,1)} %go_ref.1, bf16[768,2304]{1,0:T(8,128)(2,1)} %get-tuple-element.7.wqkv_ref, bf16[768,768]{1,0:T(8,128)(2,1)} %get-tuple-element.8.wout_ref), custom_call_target="tpu_custom_call" | custom-call | tf_op jit(solution)/shard_map/attend/pallas_call | solution.py:551
  137.0 2.1 %copy.12 = bf16[16,32,768]{2,1,0:T(8,128)(2,1)} copy(bf16[16,32,768]{2,1,0:T(8,128)(2,1)} %get-tuple-element.12) | data formatting | bytes 1572864
  139.1 1.5 %copy.13 = f32[6,2304]{1,0:T(8,128)} copy(f32[6,2304]{1,0:T(8,128)} %get-tuple-element.13) | data formatting | bytes 110592
  140.6 1.3 copy.14
